TPU v7x, 1024 devices: a whole 4x4x32 slice. The times are simulated.
1024 devices in a mesh: gx: 32 (over y, x, core), gy: 8 (over z_lo), gz: 4 (over z_hi).
Axes of the slice: x: 4, y: 4, z: 32 (z_hi: 4, z_lo: 8; z = z_hi * 8 + z_lo), core: 2. Of those that a mesh axis runs over, the one named last changes fastest.
Arguments:
- initial: float32 [256, 64, 512], P('gx', 'gy', 'gz'), may hold values from -6 to 6
- source: float32 [256, 64, 512], P('gx', 'gy', 'gz'), may hold values from -6 to 6
- metric: float32 [3, 256, 64, 512], P(None, 'gx', 'gy', 'gz'), may hold values from 0.005 to 0.05
- eigenvectors: float32 [3, 10, 10, 32, 8, 64], P(None, None, None, 'gx', 'gy', 'gz'), may hold values from -2 to 2
- eigenvalues: float32 [3, 10, 32, 8, 64], P(None, None, 'gx', 'gy', 'gz'), may hold values from 1 to 8
Outputs:
- solution: float32 [256, 64, 512], P('gx', 'gy', 'gz')
All inputs are finite; a program needn't handle non-finite values.
Results may differ from a plain program's by a relative error of at most 0.0001.
Values sent between devices are 32-bit elements; how exact they have to be, the bound alone decides.
A program may use at most 32 MiB of HBM per device.

v0:
```python
import jax
import jax.numpy as jnp
import numpy as np
from jax import lax
from jax.sharding import PartitionSpec as P

gll_points = np.array(
    [
        -1.0,
        -0.8717401485096066,
        -0.5917001814331423,
        -0.2092992179024789,
        0.2092992179024789,
        0.5917001814331423,
        0.8717401485096066,
        1.0,
    ]
)


def extended_2(value, sides, width):
    for axis, dim in sides:
        size, length = (lax.axis_size(axis), value.shape[dim])
        up = [(i, (i + 1) % size) for i in range(size - 1)]
        down = [(j, i) for i, j in up]
        last = lax.slice_in_dim(value, length - width, length, axis=dim)
        first = lax.slice_in_dim(value, 0, width, axis=dim)
        before = lax.ppermute(last, axis, up)
        after = lax.ppermute(first, axis, down)
        value = jnp.concatenate([before, value, after], axis=dim)
    return value


def derivative_table():
    number = gll_points.shape[0]
    products = np.array(
        [
            np.prod(
                [
                    gll_points[row_index] - gll_points[other]
                    for other in range(number)
                    if other != row_index
                ]
            )
            for row_index in range(number)
        ]
    )
    matrix_out = np.zeros((number, number))
    for row_index in range(number):
        for col_index in range(number):
            if row_index != col_index:
                matrix_out[row_index, col_index] = (
                    products[row_index]
                    / products[col_index]
                    / (gll_points[row_index] - gll_points[col_index])
                )
        matrix_out[row_index, row_index] = -np.sum(matrix_out[row_index])
    return matrix_out


def apply_along(values, matrix, direction):
    block_size = matrix.shape[1]
    old_shape = values.shape
    pieces_shape = (
        old_shape[:direction]
        + (old_shape[direction] // block_size, block_size)
        + old_shape[direction + 1 :]
    )
    result = jnp.tensordot(
        values.reshape(pieces_shape),
        matrix,
        axes=((direction + 1,), (1,)),
        precision=lax.Precision.HIGHEST,
    )
    result = jnp.moveaxis(result, -1, direction + 1)
    return result.reshape(
        old_shape[:direction]
        + (old_shape[direction] // block_size * matrix.shape[0],)
        + old_shape[direction + 1 :]
    )


def apply_operator(values, metric):
    deriv_table = jnp.asarray(derivative_table(), jnp.float32)
    summed = jnp.zeros_like(values)
    for direction in range(3):
        gradient = apply_along(values, deriv_table, direction)
        summed = summed + apply_along(metric[direction] * gradient, deriv_table.T, direction)
    return summed


def assemble(padded, offset):
    result = padded
    for direction in range(3):
        length = result.shape[direction]
        view_shape = [1, 1, 1]
        view_shape[direction] = length
        node_index = ((jnp.arange(length) - offset) % 8).reshape(view_shape)
        edge_zero = jnp.zeros_like(lax.slice_in_dim(result, 0, 1, axis=direction))
        upward = jnp.concatenate(
            [lax.slice_in_dim(result, 1, length, axis=direction), edge_zero], axis=direction
        )
        downward = jnp.concatenate(
            [edge_zero, lax.slice_in_dim(result, 0, length - 1, axis=direction)], axis=direction
        )
        result = (
            result
            + jnp.where(node_index == 7, upward, 0.0)
            + jnp.where(node_index == 0, downward, 0.0)
        )
    return result


def extend_axis(padded, direction):
    shifted = jnp.moveaxis(padded, direction, 0)
    blocks = (shifted.shape[0] - 4) // 8
    trailing = shifted.shape[1:]
    middle = shifted[2:-2].reshape((blocks, 8) + trailing)
    lowest = shifted[0 : 8 * blocks : 8][:, None]
    beyond = shifted[11::8][:, None]
    joined = jnp.concatenate([lowest, middle, beyond], axis=1).reshape((blocks * 10,) + trailing)
    return jnp.moveaxis(joined, 0, direction)


def widen(padded):
    return extend_axis(extend_axis(extend_axis(padded, 0), 1), 2)


def fast_solve(extended, eigenvectors, eigenvalues):
    count_x, count_y, count_z = eigenvectors.shape[3:]
    precise = lax.Precision.HIGHEST
    spectral = extended.reshape(count_x, 10, count_y, 10, count_z, 10)
    spectral = jnp.einsum("apxyz,xaybzc->xpybzc", eigenvectors[0], spectral, precision=precise)
    spectral = jnp.einsum("bqxyz,xpybzc->xpyqzc", eigenvectors[1], spectral, precision=precise)
    spectral = jnp.einsum("csxyz,xpyqzc->xpyqzs", eigenvectors[2], spectral, precision=precise)
    rate_x = jnp.transpose(eigenvalues[0], (1, 0, 2, 3))[:, :, :, None, :, None]
    rate_y = jnp.transpose(eigenvalues[1], (1, 2, 0, 3))[:, None, :, :, :, None]
    rate_z = jnp.transpose(eigenvalues[2], (1, 2, 3, 0))[:, None, :, None, :, :]
    spectral = spectral / (rate_x + rate_y + rate_z)
    spectral = jnp.einsum("csxyz,xpyqzs->xpyqzc", eigenvectors[2], spectral, precision=precise)
    spectral = jnp.einsum("bqxyz,xpyqzc->xpybzc", eigenvectors[1], spectral, precision=precise)
    spectral = jnp.einsum("apxyz,xpybzc->xaybzc", eigenvectors[0], spectral, precision=precise)
    return spectral.reshape(count_x * 10, count_y * 10, count_z * 10)


def return_axis(padded, direction):
    shifted = jnp.moveaxis(padded, direction, 0)
    blocks = (shifted.shape[0] - 4) // 10
    trailing = shifted.shape[1:]
    owned = shifted[2:-2].reshape((blocks, 10) + trailing)[:, 1:9]
    before = shifted[0 : 10 * blocks].reshape((blocks, 10) + trailing)[:, 0:2]
    following = shifted[4:].reshape((blocks, 10) + trailing)[:, 8:10]
    middle = jnp.zeros((blocks, 4) + trailing, shifted.dtype)
    summed = owned + jnp.concatenate([before, middle, following], axis=1)
    return jnp.moveaxis(summed.reshape((blocks * 8,) + trailing), 0, direction)


def body(initial, source, metric, eigenvectors, eigenvalues):
    solution = initial
    local_res = source - apply_operator(solution, metric)
    narrow = extended_2(local_res, (("gx", 0), ("gy", 1), ("gz", 2)), 1)
    assembled = assemble(narrow, 1)[1:-1, 1:-1, 1:-1]
    widened = extended_2(assembled, (("gx", 0), ("gy", 1), ("gz", 2)), 2)
    extended = widen(widened)
    corrected = fast_solve(extended, eigenvectors, eigenvalues)
    padded = extended_2(corrected, (("gx", 0), ("gy", 1), ("gz", 2)), 2)
    correction = return_axis(return_axis(return_axis(padded, 0), 1), 2)
    solution = solution + correction
    return solution


def solution(mesh):
    placed = (
        P("gx", "gy", "gz"),
        P("gx", "gy", "gz"),
        P(None, "gx", "gy", "gz"),
        P(None, None, None, "gx", "gy", "gz"),
        P(None, None, "gx", "gy", "gz"),
    )
    return jax.shard_map(
        body, mesh=mesh, in_specs=placed, out_specs=P("gx", "gy", "gz"), check_vma=False
    )
```

profile of v0, /device:TPU:7, one launch (start us, length us, event | category | flops | bytes accessed | tf_op | source)
XLA Modules:
  0.0 192.2 jit_solution(2403982268999787100)
XLA Ops:
  0.0 0.8 fusion.34
  1.1 1.1 reshape.226
  2.2 1.2 fusion.4
  3.4 0.5 fusion.40
  4.3 0.9 fusion.11
  5.8 3.7 %collective-permute-start = (f32[1,8,128]{2,0,1:T(1,128)S(1)}, f32[1,8,128]{2,0,1:T(1,128)S(1)}, u32[]{:S(2)}, u32[]{:S(2)}) collective-permute-start(f32[1,8,128]{2,0,1:T(1,128)S(1)} %get-tuple-element.45), channel_id=1, source_target_pairs={{0,32},{32,64},{64,96},{96,128},{128,160},{160,192},{192,224},{224... | collective-permute-start | bytes 12296 | tf_op jit(solution)/shard_map/ppermute | solution.py:28
  9.5 1.9 collective-permute-start.1
  11.5 5.1 %collective-permute-done.1 = f32[1,8,128]{2,0,1:T(1,128)S(1)} collective-permute-done((f32[1,8,128]{2,0,1:T(1,128)S(1)}, f32[1,8,128]{2,0,1:T(1,128)S(1)}, u32[]{:S(2)}, u32[]{:S(2)}) %collective-permute-start.1) | collective-permute-done | bytes 4128 | tf_op jit(solution)/shard_map/ppermute | solution.py:29
  16.6 3.5 %collective-permute-start.2 = (f32[10,1,128]{2,0,1:T(8,128)S(1)}, f32[10,1,128]{2,0,1:T(8,128)S(1)}, u32[]{:S(2)}, u32[]{:S(2)}) collective-permute-start(f32[10,1,128]{2,0,1:T(8,128)S(1)} %get-tuple-element.43), channel_id=1, source_target_pairs={{0,4},{4,8},{8,12},{12,16},{16,20},{20,24},{24,28},{1,5},{5,9},{9,... | collective-permute-start | bytes 15368 | tf_op jit(solution)/shard_map/ppermute | solution.py:28
  20.1 1.3 collective-permute-start.3
  21.4 3.3 %collective-permute-done.3 = f32[10,1,128]{2,0,1:T(8,128)S(1)} collective-permute-done((f32[10,1,128]{2,0,1:T(8,128)S(1)}, f32[10,1,128]{2,0,1:T(8,128)S(1)}, u32[]{:S(2)}, u32[]{:S(2)}) %collective-permute-start.3) | collective-permute-done | bytes 5152 | tf_op jit(solution)/shard_map/ppermute | solution.py:29
  24.8 15.4 %collective-permute-start.4 = (f32[10,10,1]{2,0,1:T(8,128)S(1)}, f32[10,10,1]{2,0,1:T(8,128)S(1)}, u32[]{:S(2)}, u32[]{:S(2)}) collective-permute-start(f32[10,10,1]{2,0,1:T(8,128)S(1)} %get-tuple-element.36), channel_id=1, source_target_pairs={{0,1},{1,2},{2,3},{4,5},{5,6},{6,7},{8,9},{9,10},{10,11},{12,13},{... | collective-permute-start | bytes 1208 | tf_op jit(solution)/shard_map/ppermute | solution.py:28
  40.3 1.3 collective-permute-start.5
  41.7 23.7 %collective-permute-done.5 = f32[10,10,1]{2,0,1:T(8,128)S(1)} collective-permute-done((f32[10,10,1]{2,0,1:T(8,128)S(1)}, f32[10,10,1]{2,0,1:T(8,128)S(1)}, u32[]{:S(2)}, u32[]{:S(2)}) %collective-permute-start.5) | collective-permute-done | bytes 432 | tf_op jit(solution)/shard_map/ppermute | solution.py:29
  66.3 2.4 %collective-permute-start.6 = (f32[2,8,128]{2,0,1:T(2,128)S(1)}, f32[2,8,128]{2,0,1:T(2,128)S(1)}, u32[]{:S(2)}, u32[]{:S(2)}) collective-permute-start(f32[2,8,128]{2,0,1:T(2,128)S(1)} %get-tuple-element.18), channel_id=1, source_target_pairs={{0,32},{32,64},{64,96},{96,128},{128,160},{160,192},{192,224},{224... | collective-permute-start | bytes 24584 | tf_op jit(solution)/shard_map/ppermute | solution.py:28
  68.7 1.9 %collective-permute-start.7 = (f32[2,8,128]{2,0,1:T(2,128)S(1)}, f32[2,8,128]{2,0,1:T(2,128)S(1)}, u32[]{:S(2)}, u32[]{:S(2)}) collective-permute-start(f32[2,8,128]{2,0,1:T(2,128)S(1)} %get-tuple-element.19), channel_id=1, source_target_pairs={{32,0},{64,32},{96,64},{128,96},{160,128},{192,160},{224,192},{256... | collective-permute-start | bytes 24584 | tf_op jit(solution)/shard_map/ppermute | solution.py:29
  70.8 5.0 %collective-permute-done.7 = f32[2,8,128]{2,0,1:T(2,128)S(1)} collective-permute-done((f32[2,8,128]{2,0,1:T(2,128)S(1)}, f32[2,8,128]{2,0,1:T(2,128)S(1)}, u32[]{:S(2)}, u32[]{:S(2)}) %collective-permute-start.7) | collective-permute-done | bytes 8224 | tf_op jit(solution)/shard_map/ppermute | solution.py:29
  75.8 2.5 %collective-permute-start.8 = (f32[12,2,128]{2,0,1:T(8,128)S(1)}, f32[12,2,128]{2,0,1:T(8,128)S(1)}, u32[]{:S(2)}, u32[]{:S(2)}) collective-permute-start(f32[12,2,128]{2,0,1:T(8,128)S(1)} %get-tuple-element.41), channel_id=1, source_target_pairs={{0,4},{4,8},{8,12},{12,16},{16,20},{20,24},{24,28},{1,5},{5,9},{9,... | collective-permute-start | bytes 36872 | tf_op jit(solution)/shard_map/ppermute | solution.py:28
  78.3 1.3 collective-permute-start.9
  79.8 3.1 %collective-permute-done.9 = f32[12,2,128]{2,0,1:T(8,128)S(1)} collective-permute-done((f32[12,2,128]{2,0,1:T(8,128)S(1)}, f32[12,2,128]{2,0,1:T(8,128)S(1)}, u32[]{:S(2)}, u32[]{:S(2)}) %collective-permute-start.9) | collective-permute-done | bytes 12320 | tf_op jit(solution)/shard_map/ppermute | solution.py:29
  83.0 14.3 %collective-permute-start.10 = (f32[12,12,2]{2,0,1:T(8,128)S(1)}, f32[12,12,2]{2,0,1:T(8,128)S(1)}, u32[]{:S(2)}, u32[]{:S(2)}) collective-permute-start(f32[12,12,2]{2,0,1:T(8,128)S(1)} %get-tuple-element.32), channel_id=1, source_target_pairs={{0,1},{1,2},{2,3},{4,5},{5,6},{6,7},{8,9},{9,10},{10,11},{12,13},{... | collective-permute-start | bytes 3464 | tf_op jit(solution)/shard_map/ppermute | solution.py:28
  97.3 1.5 collective-permute-start.11
  98.8 0.8 broadcast_add_fusion
  99.7 0.8 copy.80
  100.5 0.8 copy.81
  101.3 19.9 %collective-permute-done.11 = f32[12,12,2]{2,0,1:T(8,128)S(1)} collective-permute-done((f32[12,12,2]{2,0,1:T(8,128)S(1)}, f32[12,12,2]{2,0,1:T(8,128)S(1)}, u32[]{:S(2)}, u32[]{:S(2)}) %collective-permute-start.11) | collective-permute-done | bytes 1184 | tf_op jit(solution)/shard_map/ppermute | solution.py:29
  122.9 0.7 copy.41
  123.6 0.7 copy.42
  124.2 0.5 pad_maximum_fusion
  125.6 2.6 %convolution_bitcast_fusion.5 = f32[10,10,16,10]{0,3,1,2:T(8,128)S(1)} fusion(f32[10,10,16,10]{3,2,1,0:T(8,128)S(1)} %reshape.234, f32[1,10,10,1,1,16]{2,1,5,4,3,0:T(8,128)S(1)} %copy.79), kind=kOutput, calls=%fused_computation.5 | convolution fusion | flops 1920000 | bytes 134400 | tf_op jit(solution)/shard_map/apxyz,xaybzc->xpybzc/dot_general | solution.py:133
  128.2 1.6 copy.46
  129.9 1.2 convolution_bitcast_fusion.4
  131.2 2.2 %convolution_bitcast_fusion.3 = f32[1,10,1,10,16,10]{5,3,1,4,2,0:T(8,128)S(1)} fusion(f32[10,10,16,10]{1,3,0,2:T(8,128)S(1)} %convolution_bitcast_fusion.4, f32[1,10,10,1,1,16]{2,1,5,4,3,0:T(8,128)S(1)} %copy-done.5), kind=kOutput, calls=%fused_computation.3 | convolution fusion | flops 1920000 | bytes 134400 | tf_op jit(solution)/shard_map/csxyz,xpyqzc->xpyqzs/dot_general | solution.py:135
  133.4 1.5 convolution_bitcast_fusion.2
  134.9 2.4 %convolution_bitcast_fusion.1 = f32[10,10,16,10]{1,3,0,2:T(8,128)S(1)} fusion(f32[10,10,16,10]{3,1,0,2:T(8,128)S(1)} %convolution_bitcast_fusion.2, f32[1,10,10,1,1,16]{2,1,5,4,3,0:T(8,128)S(1)} %copy-done.3), kind=kOutput, calls=%fused_computation.1 | convolution fusion | flops 1920000 | bytes 134400 | tf_op jit(solution)/shard_map/bqxyz,xpyqzc->xpybzc/dot_general | solution.py:141
  137.3 1.6 copy.53
  139.0 1.2 convolution_bitcast_fusion
  140.4 3.2 %collective-permute-start.12 = (f32[2,10,160]{2,0,1:T(2,128)S(1)}, f32[2,10,160]{2,0,1:T(2,128)S(1)}, u32[]{:S(2)}, u32[]{:S(2)}) collective-permute-start(f32[2,10,160]{2,0,1:T(2,128)S(1)} %slice.236), channel_id=1, source_target_pairs={{0,32},{32,64},{64,96},{96,128},{128,160},{160,192},{192,224},{224... | collective-permute-start | bytes 38408 | tf_op jit(solution)/shard_map/ppermute | solution.py:28
  144.7 1.9 collective-permute-start.13
  146.7 5.4 %collective-permute-done.13 = f32[2,10,160]{2,1,0:T(8,128)S(1)} collective-permute-done((f32[2,10,160]{2,1,0:T(8,128)S(1)}, f32[2,10,160]{2,1,0:T(8,128)S(1)}, u32[]{:S(2)}, u32[]{:S(2)}) %collective-permute-start.13) | collective-permute-done | bytes 12832 | tf_op jit(solution)/shard_map/ppermute | solution.py:29
  152.1 1.3 collective-permute-start.14
  153.4 1.3 collective-permute-start.15
  154.7 3.3 %collective-permute-done.15 = f32[14,2,160]{2,1,0:T(2,128)S(1)} collective-permute-done((f32[14,2,160]{2,1,0:T(2,128)S(1)}, f32[14,2,160]{2,1,0:T(2,128)S(1)}, u32[]{:S(2)}, u32[]{:S(2)}) %collective-permute-start.15) | collective-permute-done | bytes 17952 | tf_op jit(solution)/shard_map/ppermute | solution.py:29
  158.1 4.4 %collective-permute-start.16 = (f32[14,14,2]{2,1,0:T(8,128)S(1)}, f32[14,14,2]{2,1,0:T(8,128)S(1)}, u32[]{:S(2)}, u32[]{:S(2)}) collective-permute-start(f32[14,14,2]{2,1,0:T(8,128)S(1)} %get-tuple-element.12), channel_id=1, source_target_pairs={{0,1},{1,2},{2,3},{4,5},{5,6},{6,7},{8,9},{9,10},{10,11},{12,13},{... | collective-permute-start | bytes 4712 | tf_op jit(solution)/shard_map/ppermute | solution.py:28
  162.6 1.3 collective-permute-start.17
  164.0 1.2 collective-permute-done.16
  165.2 24.0 %collective-permute-done.17 = f32[14,14,2]{2,1,0:T(8,128)S(1)} collective-permute-done((f32[14,14,2]{2,1,0:T(8,128)S(1)}, f32[14,14,2]{2,1,0:T(8,128)S(1)}, u32[]{:S(2)}, u32[]{:S(2)}) %collective-permute-start.17) | collective-permute-done | bytes 1600 | tf_op jit(solution)/shard_map/ppermute | solution.py:29
  191.6 0.6 bitcast_add_fusion
  (106 shorter events, 9.1 us)
Async XLA Ops:
  0.8 2.6 %copy-start.10 = (f32[8,8,1,1]{1,0,3,2:T(8,128)S(1)}, f32[8,8,1,1]{1,0,3,2:T(8,128)}, u32[]{:S(2)}) copy-start(f32[8,8,1,1]{1,0,3,2:T(8,128)} %constant.68) | copy-start | bytes 772
  2.1 2.1 %copy-start.4 = (f32[8,8,128]{2,1,0:T(8,128)S(1)}, f32[8,8,128]{2,1,0:T(8,128)}, u32[]{:S(2)}) copy-start(f32[8,8,128]{2,1,0:T(8,128)} %param.6) | copy-start | bytes 98308
  2.2 2.1 %copy-start.8 = (f32[8,8,1]{1,0,2:T(8,128)S(1)}, f32[8,8,1]{1,0,2:T(8,128)}, u32[]{:S(2)}) copy-start(f32[8,8,1]{1,0,2:T(8,128)} %constant.67) | copy-start | bytes 772
  3.4 2.2 %copy-start.9 = (f32[8,8,128]{2,1,0:T(8,128)S(1)}, f32[8,8,128]{2,1,0:T(8,128)}, u32[]{:S(2)}) copy-start(f32[8,8,128]{2,1,0:T(8,128)} %param.7) | copy-start | bytes 98308
  5.8 5.6 %collective-permute-start = (f32[1,8,128]{2,0,1:T(1,128)S(1)}, f32[1,8,128]{2,0,1:T(1,128)S(1)}, u32[]{:S(2)}, u32[]{:S(2)}) collective-permute-start(f32[1,8,128]{2,0,1:T(1,128)S(1)} %get-tuple-element.45), channel_id=1, source_target_pairs={{0,32},{32,64},{64,96},{96,128},{128,160},{160,192},{192,224},{224... | collective-permute-start | bytes 12296 | tf_op jit(solution)/shard_map/ppermute | solution.py:28
  9.5 7.0 %collective-permute-start.1 = (f32[1,8,128]{2,0,1:T(1,128)S(1)}, f32[1,8,128]{2,0,1:T(1,128)S(1)}, u32[]{:S(2)}, u32[]{:S(2)}) collective-permute-start(f32[1,8,128]{2,0,1:T(1,128)S(1)} %get-tuple-element.46), channel_id=1, source_target_pairs={{32,0},{64,32},{96,64},{128,96},{160,128},{192,160},{224,192},{256... | collective-permute-start | bytes 12296 | tf_op jit(solution)/shard_map/ppermute | solution.py:29
  16.6 4.9 %collective-permute-start.2 = (f32[10,1,128]{2,0,1:T(8,128)S(1)}, f32[10,1,128]{2,0,1:T(8,128)S(1)}, u32[]{:S(2)}, u32[]{:S(2)}) collective-permute-start(f32[10,1,128]{2,0,1:T(8,128)S(1)} %get-tuple-element.43), channel_id=1, source_target_pairs={{0,4},{4,8},{8,12},{12,16},{16,20},{20,24},{24,28},{1,5},{5,9},{9,... | collective-permute-start | bytes 15368 | tf_op jit(solution)/shard_map/ppermute | solution.py:28
  20.1 4.6 %collective-permute-start.3 = (f32[10,1,128]{2,0,1:T(8,128)S(1)}, f32[10,1,128]{2,0,1:T(8,128)S(1)}, u32[]{:S(2)}, u32[]{:S(2)}) collective-permute-start(f32[10,1,128]{2,0,1:T(8,128)S(1)} %get-tuple-element.44), channel_id=1, source_target_pairs={{4,0},{8,4},{12,8},{16,12},{20,16},{24,20},{28,24},{5,1},{9,5},{13... | collective-permute-start | bytes 15368 | tf_op jit(solution)/shard_map/ppermute | solution.py:29
  24.8 16.9 %collective-permute-start.4 = (f32[10,10,1]{2,0,1:T(8,128)S(1)}, f32[10,10,1]{2,0,1:T(8,128)S(1)}, u32[]{:S(2)}, u32[]{:S(2)}) collective-permute-start(f32[10,10,1]{2,0,1:T(8,128)S(1)} %get-tuple-element.36), channel_id=1, source_target_pairs={{0,1},{1,2},{2,3},{4,5},{5,6},{6,7},{8,9},{9,10},{10,11},{12,13},{... | collective-permute-start | bytes 1208 | tf_op jit(solution)/shard_map/ppermute | solution.py:28
  40.3 25.2 %collective-permute-start.5 = (f32[10,10,1]{2,0,1:T(8,128)S(1)}, f32[10,10,1]{2,0,1:T(8,128)S(1)}, u32[]{:S(2)}, u32[]{:S(2)}) collective-permute-start(f32[10,10,1]{2,0,1:T(8,128)S(1)} %get-tuple-element.37), channel_id=1, source_target_pairs={{1,0},{2,1},{3,2},{5,4},{6,5},{7,6},{9,8},{10,9},{11,10},{13,12},{... | collective-permute-start | bytes 1208 | tf_op jit(solution)/shard_map/ppermute | solution.py:29
  65.9 4.8 %copy-start.6 = (f32[3,10,10,1,1,16]{5,4,3,2,1,0:T(1,128)S(1)}, f32[3,10,10,1,1,16]{5,4,3,2,1,0:T(1,128)}, u32[]{:S(2)}) copy-start(f32[3,10,10,1,1,16]{5,4,3,2,1,0:T(1,128)} %param.9) | copy-start | bytes 57604
  65.9 13.7 %copy-start.11 = (f32[3,10,1,1,16]{4,3,2,1,0:T(1,128)S(1)}, f32[3,10,1,1,16]{4,3,2,1,0:T(1,128)}, u32[]{:S(2)}) copy-start(f32[3,10,1,1,16]{4,3,2,1,0:T(1,128)} %param.10) | copy-start | bytes 5764
  66.3 4.5 %collective-permute-start.6 = (f32[2,8,128]{2,0,1:T(2,128)S(1)}, f32[2,8,128]{2,0,1:T(2,128)S(1)}, u32[]{:S(2)}, u32[]{:S(2)}) collective-permute-start(f32[2,8,128]{2,0,1:T(2,128)S(1)} %get-tuple-element.18), channel_id=1, source_target_pairs={{0,32},{32,64},{64,96},{96,128},{128,160},{160,192},{192,224},{224... | collective-permute-start | bytes 24584 | tf_op jit(solution)/shard_map/ppermute | solution.py:28
  68.7 7.1 %collective-permute-start.7 = (f32[2,8,128]{2,0,1:T(2,128)S(1)}, f32[2,8,128]{2,0,1:T(2,128)S(1)}, u32[]{:S(2)}, u32[]{:S(2)}) collective-permute-start(f32[2,8,128]{2,0,1:T(2,128)S(1)} %get-tuple-element.19), channel_id=1, source_target_pairs={{32,0},{64,32},{96,64},{128,96},{160,128},{192,160},{224,192},{256... | collective-permute-start | bytes 24584 | tf_op jit(solution)/shard_map/ppermute | solution.py:29
  75.8 4.0 %collective-permute-start.8 = (f32[12,2,128]{2,0,1:T(8,128)S(1)}, f32[12,2,128]{2,0,1:T(8,128)S(1)}, u32[]{:S(2)}, u32[]{:S(2)}) collective-permute-start(f32[12,2,128]{2,0,1:T(8,128)S(1)} %get-tuple-element.41), channel_id=1, source_target_pairs={{0,4},{4,8},{8,12},{12,16},{16,20},{20,24},{24,28},{1,5},{5,9},{9,... | collective-permute-start | bytes 36872 | tf_op jit(solution)/shard_map/ppermute | solution.py:28
  78.3 4.6 %collective-permute-start.9 = (f32[12,2,128]{2,0,1:T(8,128)S(1)}, f32[12,2,128]{2,0,1:T(8,128)S(1)}, u32[]{:S(2)}, u32[]{:S(2)}) collective-permute-start(f32[12,2,128]{2,0,1:T(8,128)S(1)} %get-tuple-element.42), channel_id=1, source_target_pairs={{4,0},{8,4},{12,8},{16,12},{20,16},{24,20},{28,24},{5,1},{9,5},{13... | collective-permute-start | bytes 36872 | tf_op jit(solution)/shard_map/ppermute | solution.py:29
  83.0 18.4 %collective-permute-start.10 = (f32[12,12,2]{2,0,1:T(8,128)S(1)}, f32[12,12,2]{2,0,1:T(8,128)S(1)}, u32[]{:S(2)}, u32[]{:S(2)}) collective-permute-start(f32[12,12,2]{2,0,1:T(8,128)S(1)} %get-tuple-element.32), channel_id=1, source_target_pairs={{0,1},{1,2},{2,3},{4,5},{5,6},{6,7},{8,9},{9,10},{10,11},{12,13},{... | collective-permute-start | bytes 3464 | tf_op jit(solution)/shard_map/ppermute | solution.py:28
  97.3 24.0 %collective-permute-start.11 = (f32[12,12,2]{2,0,1:T(8,128)S(1)}, f32[12,12,2]{2,0,1:T(8,128)S(1)}, u32[]{:S(2)}, u32[]{:S(2)}) collective-permute-start(f32[12,12,2]{2,0,1:T(8,128)S(1)} %get-tuple-element.33), channel_id=1, source_target_pairs={{1,0},{2,1},{3,2},{5,4},{6,5},{7,6},{9,8},{10,9},{11,10},{13,12},{... | collective-permute-start | bytes 3464 | tf_op jit(solution)/shard_map/ppermute | solution.py:29
  99.7 25.9 %copy-start = (f32[1,10,10,1,1,16]{2,1,5,4,3,0:T(8,128)}, f32[1,10,10,1,1,16]{2,1,5,4,3,0:T(8,128)S(1)}, u32[]{:S(2)}) copy-start(f32[1,10,10,1,1,16]{2,1,5,4,3,0:T(8,128)S(1)} %copy.79) | copy-start | bytes 19204
  128.2 1.7 copy-start.2
  129.9 1.3 copy-start.5
  131.1 2.2 %copy-start.7 = (f32[10,10,16]{1,0,2:T(8,128)S(1)}, f32[10,10,16]{1,0,2:T(8,128)}, u32[]{:S(2)}) copy-start(f32[10,10,16]{1,0,2:T(8,128)} %broadcast_add_fusion) | copy-start | bytes 19204
  133.4 1.5 copy-start.3
  137.3 1.6 copy-start.1
  140.4 6.2 %collective-permute-start.12 = (f32[2,10,160]{2,0,1:T(2,128)S(1)}, f32[2,10,160]{2,0,1:T(2,128)S(1)}, u32[]{:S(2)}, u32[]{:S(2)}) collective-permute-start(f32[2,10,160]{2,0,1:T(2,128)S(1)} %slice.236), channel_id=1, source_target_pairs={{0,32},{32,64},{64,96},{96,128},{128,160},{160,192},{192,224},{224... | collective-permute-start | bytes 38408 | tf_op jit(solution)/shard_map/ppermute | solution.py:28
  144.7 7.3 %collective-permute-start.13 = (f32[2,10,160]{2,1,0:T(8,128)S(1)}, f32[2,10,160]{2,1,0:T(8,128)S(1)}, u32[]{:S(2)}, u32[]{:S(2)}) collective-permute-start(f32[2,10,160]{2,1,0:T(8,128)S(1)} %reshape.264), channel_id=1, source_target_pairs={{32,0},{64,32},{96,64},{128,96},{160,128},{192,160},{224,192},{256... | collective-permute-start | bytes 38408 | tf_op jit(solution)/shard_map/ppermute | solution.py:29
  152.1 2.6 %collective-permute-start.14 = (f32[14,2,160]{2,1,0:T(2,128)S(1)}, f32[14,2,160]{2,1,0:T(2,128)S(1)}, u32[]{:S(2)}, u32[]{:S(2)}) collective-permute-start(f32[14,2,160]{2,1,0:T(2,128)S(1)} %get-tuple-element.14), channel_id=1, source_target_pairs={{0,4},{4,8},{8,12},{12,16},{16,20},{20,24},{24,28},{1,5},{5,9},{9,... | collective-permute-start | bytes 53768 | tf_op jit(solution)/shard_map/ppermute | solution.py:28
  153.4 4.6 %collective-permute-start.15 = (f32[14,2,160]{2,1,0:T(2,128)S(1)}, f32[14,2,160]{2,1,0:T(2,128)S(1)}, u32[]{:S(2)}, u32[]{:S(2)}) collective-permute-start(f32[14,2,160]{2,1,0:T(2,128)S(1)} %get-tuple-element.15), channel_id=1, source_target_pairs={{4,0},{8,4},{12,8},{16,12},{20,16},{24,20},{28,24},{5,1},{9,5},{13... | collective-permute-start | bytes 53768 | tf_op jit(solution)/shard_map/ppermute | solution.py:29
  158.1 7.0 %collective-permute-start.16 = (f32[14,14,2]{2,1,0:T(8,128)S(1)}, f32[14,14,2]{2,1,0:T(8,128)S(1)}, u32[]{:S(2)}, u32[]{:S(2)}) collective-permute-start(f32[14,14,2]{2,1,0:T(8,128)S(1)} %get-tuple-element.12), channel_id=1, source_target_pairs={{0,1},{1,2},{2,3},{4,5},{5,6},{6,7},{8,9},{9,10},{10,11},{12,13},{... | collective-permute-start | bytes 4712 | tf_op jit(solution)/shard_map/ppermute | solution.py:28
  162.6 26.6 %collective-permute-start.17 = (f32[14,14,2]{2,1,0:T(8,128)S(1)}, f32[14,14,2]{2,1,0:T(8,128)S(1)}, u32[]{:S(2)}, u32[]{:S(2)}) collective-permute-start(f32[14,14,2]{2,1,0:T(8,128)S(1)} %get-tuple-element.13), channel_id=1, source_target_pairs={{1,0},{2,1},{3,2},{5,4},{6,5},{7,6},{9,8},{10,9},{11,10},{13,12},{... | collective-permute-start | bytes 4712 | tf_op jit(solution)/shard_map/ppermute | solution.py:29
where the time goes:
time: 193 us; the launch traced here: 192 us
  waiting for transfers between devices  94.2 us (49%)
  starting transfers between devices  64.5 us (33%)
  local copies, waits for them, and re-layouts  14.5 us (8%)
  matrix products  14.5 us (8%)
  other arithmetic  3.66 us (2%)
    ppermute x9, waiting for transfers between devices, extended_2(): after = lax.ppermute(first, axis, down)  92.8 us
    ppermute x9, starting transfers between devices, extended_2(): before = lax.ppermute(last, axis, up)  50.7 us
    ppermute x9, starting transfers between devices, extended_2(): after = lax.ppermute(first, axis, down)  13.7 us
  transfers between devices with their start and end apart: 18, of which 11 were waited for; matrix products, arithmetic and copies ran while one was open for 2% of the time, Pallas kernels for 0%

commit v1 on v0

v1 whole, which is shorter than its diff:
```python
import functools

import jax
import jax.numpy as jnp
import numpy as np
from jax import lax
from jax.experimental import pallas as pl
from jax.experimental.pallas import tpu as pltpu
from jax.sharding import PartitionSpec as P

MESH = pl.DeviceIdType.MESH
F32 = jnp.float32
BF16 = jnp.bfloat16

gll_points = np.array(
    [
        -1.0,
        -0.8717401485096066,
        -0.5917001814331423,
        -0.2092992179024789,
        0.2092992179024789,
        0.5917001814331423,
        0.8717401485096066,
        1.0,
    ]
)

DIRS = [(-1, 0), (1, 0), (0, -1), (0, 1), (-1, -1), (-1, 1), (1, -1), (1, 1)]
OPP = [1, 0, 3, 2, 7, 6, 5, 4]
OYF, OYB, OZ, OL, ROWS = 160, 320, 480, 720, 768


def derivative_table():
    number = gll_points.shape[0]
    products = np.array(
        [
            np.prod([gll_points[i] - gll_points[k] for k in range(number) if k != i])
            for i in range(number)
        ]
    )
    table = np.zeros((number, number))
    for i in range(number):
        for j in range(number):
            if i != j:
                table[i, j] = products[i] / products[j] / (gll_points[i] - gll_points[j])
        table[i, i] = -np.sum(table[i])
    return table


def operator_tables():
    table = derivative_table().astype(np.float32)
    eye = np.eye(8, dtype=np.float32)
    left = np.concatenate([np.kron(table, eye), np.kron(eye, table)], axis=0)
    left = np.concatenate([left, np.zeros((128, 64), np.float32)], axis=1)
    left_t = np.ascontiguousarray(left.T[:64])
    right = np.kron(np.eye(16, dtype=np.float32), table.T)
    full = np.concatenate([left, left_t, right, right.T], axis=0)
    high = full.astype(jnp.bfloat16)
    low = (full - high.astype(np.float32)).astype(jnp.bfloat16)
    return np.stack([high, low])


def dot(a, b, dims=((1,), (0,))):
    return lax.dot_general(a, b, (dims, ((), ())), preferred_element_type=F32)


def halves(value):
    high = value.astype(BF16)
    return high, (value - high.astype(F32)).astype(BF16)


def thirds(value):
    high = value.astype(BF16)
    rest = value - high.astype(F32)
    mid = rest.astype(BF16)
    return high, mid, (rest - mid.astype(F32)).astype(BF16)


def dot3(a, b, dims=((1,), (0,))):
    return dot(a[0], b[0], dims) + (dot(a[1], b[0], dims) + dot(a[0], b[1], dims))


def lanes(group):
    lane = lax.broadcasted_iota(jnp.int32, (1, 128), 1)
    if group == 0:
        return lane & 15, lane >> 4
    inside, low, high = lane < 32, lane < 42, lane < 52
    element = jnp.where(inside, lane & 15, jnp.where(low, -1, jnp.where(high, 16, 99)))
    mode = jnp.where(
        inside, 8 + (lane >> 4), jnp.where(low, lane - 32, jnp.where(high, lane - 42, 99))
    )
    return element, mode


def kernel(
    nx, ny, nz,
    u_h, f_h, m_h, eig_h, lam_h, cst_h, out_ref,
    u_v, f_v, m_v, cst_v, ex, eyf, eyb, ez, el, in_sem,
    send_x, send_y, send_d, recv_x, recv_y, recv_d, near_send, near_recv,
    fe_send, fe_recv, fx_send, fx_recv, far_send, far_recv, ready,
    xs, xc, cm, cxb, inv, wh, wl, zs,
):
    ix, iy, iz = lax.axis_index("gx"), lax.axis_index("gy"), lax.axis_index("gz")

    first = [(u_h, u_v), (cst_h, cst_v), (m_h, m_v), (f_h, f_v)]
    second = [
        (eig_h.at[0, 1:9, :, 0, 0], ex.at[0:8, 0:10]),
        (eig_h.at[0, 0, :, 0, 0], ex.at[8, 0:10]),
        (eig_h.at[0, 9, :, 0, 0], ex.at[9, 0:10]),
        (eig_h.at[1, 1:9, :, 0, 0], eyf.at[0:8, 0:10]),
        (eig_h.at[1, 0, :, 0, 0], eyf.at[8, 0:10]),
        (eig_h.at[1, 9, :, 0, 0], eyf.at[9, 0:10]),
        (lam_h.at[:, :, 0, 0], el.at[:, 0:10]),
    ]
    for row, pos in enumerate([1, 2, 3, 4, 5, 6, 7, 8, 0, 9]):
        second.append((eig_h.at[1, pos, :, 0, 0], eyb.at[:, row]))
    for row, pos in enumerate([1, 2, 3, 4, 5, 6, 7, 8]):
        second.append((eig_h.at[2, pos, :, 0, 0], ez.at[:, row]))
    for row, pos in [(14, 0), (15, 1), (16, 8), (17, 9)]:
        second.append((eig_h.at[2, pos, :, 0, 0], ez.at[:, row]))
    loads = [
        pltpu.make_async_copy(src, dst, in_sem.at[i])
        for i, (src, dst) in enumerate(first + second)
    ]
    for load in loads:
        load.start()

    recv_x[...] = jnp.zeros_like(recv_x)
    recv_y[...] = jnp.zeros_like(recv_y)
    recv_d[...] = jnp.zeros_like(recv_d)
    fe_recv[...] = jnp.zeros_like(fe_recv)
    fx_recv[...] = jnp.zeros_like(fx_recv)

    half = ny // 2
    spot = iz * ny + iy
    above, below = spot + half, spot - half
    has_above, has_below = above < nz * ny, below >= 0
    below_safe = jnp.maximum(below, 0)
    to_above = (ix, above % ny, above // ny)
    to_below = (ix, below_safe % ny, below_safe // ny)
    has_next, has_prev = iz < nz - 1, iz > 0
    to_next, to_prev = (ix, iy, iz + 1), (ix, iy, iz - 1)
    near, target = [], []
    for dx, dy in DIRS:
        ok = None
        for cond in (
            [ix > 0] * (dx < 0) + [ix < nx - 1] * (dx > 0)
            + [iy > 0] * (dy < 0) + [iy < ny - 1] * (dy > 0)
        ):
            ok = cond if ok is None else ok & cond
        near.append(ok)
        target.append((ix + dx, iy + dy, iz))
    barrier = pltpu.get_barrier_semaphore()
    count = jnp.int32(0)
    for ok, device in list(zip(near, target)) + [(has_above, to_above), (has_below, to_below)]:
        @pl.when(ok)
        def _(device=device):
            pl.semaphore_signal(barrier, 1, device_id=device, device_id_type=MESH)
        count = count + ok.astype(jnp.int32)

    ex[:, 10:16, :] = jnp.zeros((10, 6, 16), F32)
    eyf[:, 10:16, :] = jnp.zeros((10, 6, 16), F32)
    eyb[:, 10:16, :] = jnp.zeros((10, 6, 16), F32)
    ez[:, 8:14, :] = jnp.zeros((10, 6, 16), F32)
    ez[:, 18:24, :] = jnp.zeros((10, 6, 16), F32)
    el[:, 10:16, :] = jnp.zeros((3, 6, 16), F32)
    xs[:, 10:16, :] = jnp.zeros((10, 6, 128), F32)
    xc[96:128, :] = jnp.zeros((32, 128), F32)

    for load in loads[:4]:
        load.wait()
    field = halves(u_v[...].reshape(64, 128))
    left = cst_v[0, 0:128, 0:64], cst_v[1, 0:128, 0:64]
    left_t = cst_v[0, 128:192], cst_v[1, 128:192]
    right = cst_v[0, 192:320], cst_v[1, 192:320]
    right_t = cst_v[0, 320:448], cst_v[1, 320:448]
    flux = dot3(left, field) * m_v[0:2].reshape(128, 128)
    flux_z = dot3(field, right) * m_v[2].reshape(64, 128)
    applied = dot3(left_t, halves(flux)) + dot3(halves(flux_z), right_t)
    res = f_v[...] - applied.reshape(8, 8, 128)

    def recv_of(turn, k):
        if k < 2:
            return recv_x.at[turn, k]
        return recv_y.at[turn, k - 2] if k < 4 else recv_d.at[turn, k - 4]

    def send_of(turn, k):
        if k < 2:
            return send_x.at[turn, k]
        return send_y.at[turn, k - 2] if k < 4 else send_d.at[turn, k - 4]

    def outgoing(turn, k):
        return pltpu.make_async_remote_copy(
            src_ref=send_of(turn, k),
            dst_ref=recv_of(turn, OPP[k]),
            send_sem=near_send.at[turn, k],
            recv_sem=near_recv.at[turn, OPP[k]],
            device_id=target[k],
            device_id_type=MESH,
        )

    def incoming(turn, k):
        return pltpu.make_async_remote_copy(
            src_ref=send_of(turn, k),
            dst_ref=recv_of(turn, k),
            send_sem=near_send.at[turn, k],
            recv_sem=near_recv.at[turn, k],
            device_id=target[k],
            device_id_type=MESH,
        )

    ORDER = [4, 5, 6, 7, 0, 1, 2, 3]

    def send_near(turn):
        for k in ORDER:
            @pl.when(near[k])
            def _(k=k):
                outgoing(turn, k).start()

    def wait_near(turn):
        for k in ORDER:
            @pl.when(near[k])
            def _(k=k):
                incoming(turn, k).wait_recv()

    def pack(turn, value, low, high):
        for side, rows in enumerate((low, high)):
            for j, row in enumerate(rows):
                send_x[turn, side, j] = value[row, 0:8]
                send_y[turn, side, :, j : j + 1, :] = value[0:8, row : row + 1]
        for k in range(4, 8):
            rows_x = low if DIRS[k][0] < 0 else high
            rows_y = low if DIRS[k][1] < 0 else high
            for i, row_x in enumerate(rows_x):
                for j, row_y in enumerate(rows_y):
                    send_d[turn, k - 4, i, j : j + 1, :] = value[row_x, row_y : row_y + 1]

    pack(0, res, (0, 1), (6, 7))
    pl.semaphore_wait(barrier, count)
    send_near(0)

    @pl.when(has_above & has_below)
    def _():
        pl.semaphore_signal(ready.at[0], 1, device_id=to_below, device_id_type=MESH)
        pl.semaphore_signal(ready.at[1], 1, device_id=to_above, device_id_type=MESH)

    for load in loads[4:]:
        load.wait()
    eigen = jnp.concatenate(
        [
            ex[...].reshape(160, 16),
            eyf[...].reshape(160, 16),
            eyb[...].reshape(160, 16),
            ez[...].reshape(240, 16),
            el[...].reshape(48, 16),
        ],
        axis=0,
    )
    parts = thirds(eigen)
    wanted = lax.broadcasted_iota(jnp.int32, (8, 16), 0) * 15
    picks = jnp.where(lax.broadcasted_iota(jnp.int32, (8, 16), 1) == wanted, 1.0, 0.0).astype(BF16)
    ends = sum(dot(picks, part, ((1,), (1,))) for part in parts)
    fe_send[0] = ends[0:1]
    fe_send[1] = ends[1:2]

    def prepare(g):
        element, mode = lanes(g)
        spread = jnp.where(
            lax.broadcasted_iota(jnp.int32, (16, 128), 0) == element, 1.0, 0.0
        ).astype(BF16)
        table = sum(dot(part, spread) for part in parts)
        if g == 1:
            row = lax.broadcasted_iota(jnp.int32, (8, ROWS), 0)
            other = jnp.where(row == 0, fe_recv[0], jnp.where(row == 1, fe_recv[1], 0.0))
            far_row = lax.broadcasted_iota(jnp.int32, (8, 128), 0)
            spread_far = jnp.where(
                ((far_row == 0) & (element == -1)) | ((far_row == 1) & (element == 16)), 1.0, 0.0
            ).astype(BF16)
            far = sum(dot(part, spread_far, ((0,), (0,))) for part in thirds(other))
            table = table + far
        cm[g] = table
        for r in range(100):
            at = 16 * (r // 10) + r % 10
            cxb[g, r // 10, r % 10] = jnp.broadcast_to(cm[g, at : at + 1, :], (8, 128))
        tiles = jnp.zeros((24, 128), F32)
        for s in range(10):
            tiles = tiles + jnp.where(mode == s, cm[g, OZ + 24 * s : OZ + 24 * s + 24, :], 0.0)
        inner, lower, upper = tiles[0:8], tiles[8:16], tiles[16:24]
        columns = []
        for e in list(range(16)) + [-2, -1, 16, 17]:
            columns.append(
                jnp.where(
                    element == e,
                    inner,
                    jnp.where(element == e + 1, lower, jnp.where(element == e - 1, upper, 0.0)),
                )
            )
        wh[g], wl[g] = halves(jnp.concatenate(columns, axis=0))
        rate_z = jnp.where(
            lax.broadcasted_iota(jnp.int32, (16, 128), 0) == mode, cm[g, OL + 32 : OL + 48, :], 0.0
        ).sum(axis=0, keepdims=True)
        rate_yz = cm[g, OL + 16 : OL + 32, :] + rate_z
        for p in range(10):
            rate = rate_yz + cm[g, OL + p : OL + p + 1, :]
            some = rate > 0.0
            inv[g, p] = jnp.where(some, 1.0 / jnp.where(some, rate, 1.0), 0.0)

    def far_copy(kind, way, arriving):
        if kind == 0:
            src, dst = fe_send.at[1 - way], fe_recv.at[way]
        else:
            src, dst = fx_send.at[way], fx_recv.at[way]
        return pltpu.make_async_remote_copy(
            src_ref=src,
            dst_ref=dst,
            send_sem=far_send.at[kind, way],
            recv_sem=far_recv.at[kind, way],
            device_id=to_next if (way == 0) != arriving else to_prev,
            device_id_type=MESH,
        )

    prepare(0)

    @pl.when(has_next)
    def _():
        pl.semaphore_wait(ready.at[0], 1)
        far_copy(0, 0, False).start()

    @pl.when(has_prev)
    def _():
        pl.semaphore_wait(ready.at[1], 1)
        far_copy(0, 1, False).start()

    wait_near(0)

    def join(own, prev, after):
        return jnp.concatenate(
            [own[0:1] + prev[1:2], own[1:7], own[7:8] + after[0:1], prev[0:1], after[1:2]], axis=0
        )

    xs[:, 0:8, :] = join(res, recv_x[0, 0], recv_x[0, 1])
    before = join(recv_y[0, 0], recv_d[0, 0], recv_d[0, 2])
    behind = join(recv_y[0, 1], recv_d[0, 1], recv_d[0, 3])
    xs[:, 0:1, :] = xs[:, 0:1, :] + before[:, 1:2]
    xs[:, 7:8, :] = xs[:, 7:8, :] + behind[:, 0:1]
    xs[:, 8:9, :] = before[:, 0:1]
    xs[:, 9:10, :] = behind[:, 1:2]
    xc[0:80, :] = xs[:, 0:8, :].reshape(80, 128)
    for a in range(10):
        xc[80 + 2 * a : 82 + 2 * a, :] = xs[a, 8:10, :]
    turned = xc[...].T
    fx_send[0] = turned[112:128]
    fx_send[1] = turned[0:16]

    @pl.when(has_next)
    def _():
        far_copy(1, 0, False).start()

    @pl.when(has_prev)
    def _():
        far_copy(1, 1, False).start()

    nodes = halves(xs[...].reshape(160, 128))

    def to_modes(g):
        zs[g] = dot3(nodes, (wh[g, 0:128], wl[g, 0:128])).reshape(10, 16, 128)

    to_modes(0)

    @pl.when(has_next)
    def _():
        far_copy(0, 1, True).wait_recv()

    @pl.when(has_prev)
    def _():
        far_copy(0, 0, True).wait_recv()

    prepare(1)
    to_modes(1)

    @pl.when(has_next)
    def _():
        far_copy(1, 1, True).wait_recv()

    @pl.when(has_prev)
    def _():
        far_copy(1, 0, True).wait_recv()

    beyond = halves(fx_recv[...].reshape(32, 128))

    def solve(g):
        more = dot3(beyond, (wh[g, 128:160], wl[g, 128:160]), ((0,), (0,)))
        zs[g, :, 0:8, :] = zs[g, :, 0:8, :] + more[0:80].reshape(10, 8, 128)
        for a in range(10):
            zs[g, a, 8:10, :] = zs[g, a, 8:10, :] + more[80 + 2 * a : 82 + 2 * a]
        value = zs[g].reshape(10, 2, 8, 128)
        total = None
        for a in range(10):
            term = cxb[g, a][:, None] * value[a][None]
            total = term if total is None else total + term
        value, total = total, None
        for b in range(10):
            row = value[:, b // 8, b % 8 : b % 8 + 1, :][:, None]
            pick = cm[g, OYF + 16 * b : OYF + 16 * b + 16, :].reshape(1, 2, 8, 128)
            term = pick * row
            total = term if total is None else total + term
        value, total = total * inv[g].reshape(10, 2, 8, 128), None
        for q in range(10):
            row = value[:, q // 8, q % 8 : q % 8 + 1, :][:, None]
            pick = cm[g, OYB + 16 * q : OYB + 16 * q + 16, :].reshape(1, 2, 8, 128)
            term = pick * row
            total = term if total is None else total + term
        value, total = total, None
        for p in range(10):
            term = cxb[g, :, p][:, None] * value[p][None]
            total = term if total is None else total + term
        return dot3(
            halves(total.reshape(160, 128)), (wh[g, 0:128], wl[g, 0:128]), ((1,), (1,))
        )

    found = (solve(0) + solve(1)).reshape(10, 16, 128)
    pack(1, found, (8, 0), (7, 9))
    send_near(1)
    wait_near(1)

    def gather(own, prev, after):
        return jnp.concatenate([own[0:2] + prev, own[2:6], own[6:8] + after], axis=0)

    out_ref[...] = gather(found[0:8, 0:8], recv_x[1, 0], recv_x[1, 1])
    out_ref[:, 0:2, :] = out_ref[:, 0:2, :] + gather(recv_y[1, 0], recv_d[1, 0], recv_d[1, 2])
    out_ref[:, 6:8, :] = out_ref[:, 6:8, :] + gather(recv_y[1, 1], recv_d[1, 1], recv_d[1, 3])

    for turn in range(2):
        for k in range(8):
            @pl.when(near[k])
            def _(turn=turn, k=k):
                outgoing(turn, k).wait_send()

    for kind in range(2):
        @pl.when(has_next)
        def _(kind=kind):
            far_copy(kind, 0, False).wait_send()

        @pl.when(has_prev)
        def _(kind=kind):
            far_copy(kind, 1, False).wait_send()


def solution(mesh):
    nx, ny, nz = mesh.shape["gx"], mesh.shape["gy"], mesh.shape["gz"]

    def body(initial, source, metric, eigenvectors, eigenvalues):
        hbm = pl.BlockSpec(memory_space=pl.ANY)
        vmem = pltpu.VMEM
        correction = pl.pallas_call(
            functools.partial(kernel, nx, ny, nz),
            out_shape=jax.ShapeDtypeStruct((8, 8, 128), F32),
            in_specs=[hbm] * 6,
            out_specs=pl.BlockSpec(memory_space=vmem),
            scratch_shapes=[
                vmem((8, 8, 128), F32),
                vmem((8, 8, 128), F32),
                vmem((3, 8, 8, 128), F32),
                vmem((2, 448, 128), BF16),
                vmem((10, 16, 16), F32),
                vmem((10, 16, 16), F32),
                vmem((10, 16, 16), F32),
                vmem((10, 24, 16), F32),
                vmem((3, 16, 16), F32),
                pltpu.SemaphoreType.DMA((33,)),
                vmem((2, 2, 2, 8, 128), F32),
                vmem((2, 2, 8, 2, 128), F32),
                vmem((2, 4, 2, 2, 128), F32),
                vmem((2, 2, 2, 8, 128), F32),
                vmem((2, 2, 8, 2, 128), F32),
                vmem((2, 4, 2, 2, 128), F32),
                pltpu.SemaphoreType.DMA((2, 8)),
                pltpu.SemaphoreType.DMA((2, 8)),
                vmem((2, 1, ROWS), F32),
                vmem((2, 1, ROWS), F32),
                vmem((2, 16, 128), F32),
                vmem((2, 16, 128), F32),
                pltpu.SemaphoreType.DMA((2, 2)),
                pltpu.SemaphoreType.DMA((2, 2)),
                pltpu.SemaphoreType.REGULAR((2,)),
                vmem((10, 16, 128), F32),
                vmem((128, 128), F32),
                vmem((2, ROWS, 128), F32),
                vmem((2, 10, 10, 8, 128), F32),
                vmem((2, 10, 16, 128), F32),
                vmem((2, 160, 128), BF16),
                vmem((2, 160, 128), BF16),
                vmem((2, 10, 16, 128), F32),
            ],
            compiler_params=pltpu.CompilerParams(collective_id=0, has_side_effects=True),
        )(
            initial,
            source,
            metric,
            eigenvectors,
            eigenvalues,
            jnp.asarray(operator_tables()),
        )
        return initial + correction

    placed = (
        P("gx", "gy", "gz"),
        P("gx", "gy", "gz"),
        P(None, "gx", "gy", "gz"),
        P(None, None, None, "gx", "gy", "gz"),
        P(None, None, "gx", "gy", "gz"),
    )
    return jax.shard_map(
        body, mesh=mesh, in_specs=placed, out_specs=P("gx", "gy", "gz"), check_vma=False
    )
```

time: 193 us -> 40.1 us (0.21)
  the two profiles are of different devices: /device:TPU:7 before, /device:TPU:1 now
where the time goes in v1:
time: 40.1 us; the launch traced here: 39.8 us
  Pallas kernels  38.4 us (96%)
  other arithmetic  1.38 us (3%)
    pallas_call x1, Pallas kernels, body(): pl.pallas_call(functools.partial(kernel, nx, ny, nz), out_shape=jax.Shape...  38.4 us
    add x1, other arithmetic, body(): return initial + correction  1.38 us

profile of v1, /device:TPU:1, one launch (start us, length us, event | category | flops | bytes accessed | tf_op | source)
XLA Modules:
  0.0 39.8 jit_solution(17909970671398028741)
XLA Ops:
  0.0 0.0 copy-start
  0.0 38.4 %shard_map.64 = f32[8,8,128]{2,1,0:T(8,128)} custom-call(f32[8,8,128]{2,1,0:T(8,128)} %u_h.1, f32[8,8,128]{2,1,0:T(8,128)} %f_h.1, f32[3,8,8,128]{3,2,1,0:T(8,128)} %m_h.1, f32[3,10,10,1,1,16]{5,4,3,2,1,0:T(1,128)} %eig_h.1, f32[3,10,1,1,16]{4,3,2,1,0:T(1,128)} %lam_h.1, bf16[2,448,128]{2,1,0:T(8,128)(2,1)} %constant.2.clone.cst_h), custom_call_target="tpu_custom_call" | custom-call | tf_op jit(solution)/shard_map/pallas_call | solution.py:455
  38.4 0.0 copy-done
  38.4 1.4 %add.3 = f32[8,8,128]{2,1,0:T(8,128)} add(f32[8,8,128]{2,1,0:T(8,128)S(1)} %copy-done, f32[8,8,128]{2,1,0:T(8,128)} %shard_map.64) | non-fusion elementwise | flops 8192 | bytes 98304 | tf_op jit(solution)/shard_map/add | solution.py:504
Async XLA Ops:
  0.0 38.4 %copy-start = (f32[8,8,128]{2,1,0:T(8,128)S(1)}, f32[8,8,128]{2,1,0:T(8,128)}, u32[]{:S(2)}) copy-start(f32[8,8,128]{2,1,0:T(8,128)} %u_h.1) | copy-start | bytes 98308

commit v2 on v1

--- a/solution.py
+++ b/solution.py
@@ -97,7 +97,7 @@
     u_h, f_h, m_h, eig_h, lam_h, cst_h, out_ref,
     u_v, f_v, m_v, cst_v, ex, eyf, eyb, ez, el, in_sem,
     send_x, send_y, send_d, recv_x, recv_y, recv_d, near_send, near_recv,
-    fe_send, fe_recv, fx_send, fx_recv, far_send, far_recv, ready,
+    fe_send, fe_recv, fx_send, fx_recv, far_send, far_recv, ready, pe, px, side_send, side_recv,
     xs, xc, cm, cxb, inv, wh, wl, zs,
 ):
     ix, iy, iz = lax.axis_index("gx"), lax.axis_index("gy"), lax.axis_index("gz")
@@ -131,15 +131,13 @@
     fe_recv[...] = jnp.zeros_like(fe_recv)
     fx_recv[...] = jnp.zeros_like(fx_recv)
 
-    half = ny // 2
-    spot = iz * ny + iy
-    above, below = spot + half, spot - half
-    has_above, has_below = above < nz * ny, below >= 0
-    below_safe = jnp.maximum(below, 0)
-    to_above = (ix, above % ny, above // ny)
-    to_below = (ix, below_safe % ny, below_safe // ny)
     has_next, has_prev = iz < nz - 1, iz > 0
     to_next, to_prev = (ix, iy, iz + 1), (ix, iy, iz - 1)
+    detour = nx > 1 and nz > 1
+    in_line = (ix == 0) & (iy == 0)
+    origin = in_line & (iz == 0) & detour
+    after_origin = in_line & (iz == 1) & detour
+    helper = (ix == 1) & (iy == 0) & (iz == 0) & detour
     near, target = [], []
     for dx, dy in DIRS:
         ok = None
@@ -152,10 +150,15 @@
         target.append((ix + dx, iy + dy, iz))
     barrier = pltpu.get_barrier_semaphore()
     count = jnp.int32(0)
-    for ok, device in list(zip(near, target)) + [(has_above, to_above), (has_below, to_below)]:
+    greeted = list(zip(near, target)) + [
+        (has_next & ~origin, to_next), (helper, (0, 0, 1)), (after_origin, (0, 0, 0))
+    ]
+    for ok, device in greeted:
         @pl.when(ok)
         def _(device=device):
             pl.semaphore_signal(barrier, 1, device_id=device, device_id_type=MESH)
+    count = jnp.int32(0)
+    for ok in near + [has_prev, origin]:
         count = count + ok.astype(jnp.int32)
 
     ex[:, 10:16, :] = jnp.zeros((10, 6, 16), F32)
@@ -239,10 +242,9 @@
     pl.semaphore_wait(barrier, count)
     send_near(0)
 
-    @pl.when(has_above & has_below)
+    @pl.when(has_prev & ~after_origin)
     def _():
-        pl.semaphore_signal(ready.at[0], 1, device_id=to_below, device_id_type=MESH)
-        pl.semaphore_signal(ready.at[1], 1, device_id=to_above, device_id_type=MESH)
+        pl.semaphore_signal(ready, 1, device_id=to_prev, device_id_type=MESH)
 
     for load in loads[4:]:
         load.wait()
@@ -305,11 +307,14 @@
             some = rate > 0.0
             inv[g, p] = jnp.where(some, 1.0 / jnp.where(some, rate, 1.0), 0.0)
 
+    def rows_of(way):
+        return pl.ds(6, 10) if way == 0 else pl.ds(0, 10)
+
     def far_copy(kind, way, arriving):
         if kind == 0:
             src, dst = fe_send.at[1 - way], fe_recv.at[way]
         else:
-            src, dst = fx_send.at[way], fx_recv.at[way]
+            src, dst = fx_send.at[way, rows_of(way)], fx_recv.at[way, rows_of(way)]
         return pltpu.make_async_remote_copy(
             src_ref=src,
             dst_ref=dst,
@@ -319,17 +324,52 @@
             device_id_type=MESH,
         )
 
+    def aside(kind, passing):
+        held = pe if kind == 0 else px
+        if passing:
+            src, dst = held, fe_recv.at[1] if kind == 0 else fx_recv.at[1, rows_of(1)]
+        else:
+            src, dst = fe_send.at[0] if kind == 0 else fx_send.at[1, rows_of(1)], held
+        return pltpu.make_async_remote_copy(
+            src_ref=src,
+            dst_ref=dst,
+            send_sem=side_send.at[kind] if passing else far_send.at[kind, 1],
+            recv_sem=far_recv.at[kind, 1] if passing else side_recv.at[kind],
+            device_id=(0, 0, 0) if passing else (1, 0, 0),
+            device_id_type=MESH,
+        )
+
+    def send_down(kind):
+        @pl.when(has_prev & ~after_origin)
+        def _():
+            far_copy(kind, 1, False).start()
+
+        @pl.when(after_origin)
+        def _():
+            aside(kind, False).start()
+
+    def send_up(kind):
+        @pl.when(has_next)
+        def _():
+            far_copy(kind, 0, False).start()
+
+    def pass_on(kind):
+        @pl.when(helper)
+        def _():
+            aside(kind, False).wait_recv()
+            aside(kind, True).start()
+
+    def wait_far(kind):
+        @pl.when(has_next)
+        def _():
+            far_copy(kind, 1, True).wait_recv()
+
+        @pl.when(has_prev)
+        def _():
+            far_copy(kind, 0, True).wait_recv()
+
+    send_down(0)
     prepare(0)
-
-    @pl.when(has_next)
-    def _():
-        pl.semaphore_wait(ready.at[0], 1)
-        far_copy(0, 0, False).start()
-
-    @pl.when(has_prev)
-    def _():
-        pl.semaphore_wait(ready.at[1], 1)
-        far_copy(0, 1, False).start()
 
     wait_near(0)
 
@@ -352,14 +392,7 @@
     fx_send[0] = turned[112:128]
     fx_send[1] = turned[0:16]
 
-    @pl.when(has_next)
-    def _():
-        far_copy(1, 0, False).start()
-
-    @pl.when(has_prev)
-    def _():
-        far_copy(1, 1, False).start()
-
+    send_down(1)
     nodes = halves(xs[...].reshape(160, 128))
 
     def to_modes(g):
@@ -367,24 +400,18 @@
 
     to_modes(0)
 
-    @pl.when(has_next)
+    @pl.when(has_next & ~origin)
     def _():
-        far_copy(0, 1, True).wait_recv()
-
-    @pl.when(has_prev)
-    def _():
-        far_copy(0, 0, True).wait_recv()
-
+        pl.semaphore_wait(ready, 1)
+
+    send_up(0)
+    send_up(1)
+    pass_on(0)
+    wait_far(0)
     prepare(1)
     to_modes(1)
-
-    @pl.when(has_next)
-    def _():
-        far_copy(1, 1, True).wait_recv()
-
-    @pl.when(has_prev)
-    def _():
-        far_copy(1, 0, True).wait_recv()
+    pass_on(1)
+    wait_far(1)
 
     beyond = halves(fx_recv[...].reshape(32, 128))
 
@@ -441,9 +468,17 @@
         def _(kind=kind):
             far_copy(kind, 0, False).wait_send()
 
-        @pl.when(has_prev)
+        @pl.when(has_prev & ~after_origin)
         def _(kind=kind):
             far_copy(kind, 1, False).wait_send()
+
+        @pl.when(after_origin)
+        def _(kind=kind):
+            aside(kind, False).wait_send()
+
+        @pl.when(helper)
+        def _(kind=kind):
+            aside(kind, True).wait_send()
 
 
 def solution(mesh):
@@ -482,7 +517,11 @@
                 vmem((2, 16, 128), F32),
                 pltpu.SemaphoreType.DMA((2, 2)),
                 pltpu.SemaphoreType.DMA((2, 2)),
-                pltpu.SemaphoreType.REGULAR((2,)),
+                pltpu.SemaphoreType.REGULAR,
+                vmem((1, ROWS), F32),
+                vmem((10, 128), F32),
+                pltpu.SemaphoreType.DMA((2,)),
+                pltpu.SemaphoreType.DMA((2,)),
                 vmem((10, 16, 128), F32),
                 vmem((128, 128), F32),
                 vmem((2, ROWS, 128), F32),

time: 40.1 us -> 34.1 us (0.85)
  the two profiles are of different devices: /device:TPU:1 before, /device:TPU:79 now
where the time goes in v2:
time: 34.1 us; the launch traced here: 33.8 us
  Pallas kernels  32.4 us (95%)
  other arithmetic  1.38 us (4%)
    pallas_call x1, Pallas kernels, body(): pl.pallas_call(functools.partial(kernel, nx, ny, nz), out_shape=jax.Shape...  32.4 us
    add x1, other arithmetic, body(): return initial + correction  1.38 us

profile of v2, /device:TPU:79, one launch (start us, length us, event | category | flops | bytes accessed | tf_op | source)
XLA Modules:
  0.0 33.8 jit_solution(10695825776530878471)
XLA Ops:
  0.0 0.0 copy-start
  0.0 32.4 %shard_map.64 = f32[8,8,128]{2,1,0:T(8,128)} custom-call(f32[8,8,128]{2,1,0:T(8,128)} %u_h.1, f32[8,8,128]{2,1,0:T(8,128)} %f_h.1, f32[3,8,8,128]{3,2,1,0:T(8,128)} %m_h.1, f32[3,10,10,1,1,16]{5,4,3,2,1,0:T(1,128)} %eig_h.1, f32[3,10,1,1,16]{4,3,2,1,0:T(1,128)} %lam_h.1, bf16[2,448,128]{2,1,0:T(8,128)(2,1)} %constant.2.clone.cst_h), custom_call_target="tpu_custom_call" | custom-call | tf_op jit(solution)/shard_map/pallas_call | solution.py:490
  32.4 0.0 copy-done
  32.4 1.4 %add.3 = f32[8,8,128]{2,1,0:T(8,128)} add(f32[8,8,128]{2,1,0:T(8,128)S(1)} %copy-done, f32[8,8,128]{2,1,0:T(8,128)} %shard_map.64) | non-fusion elementwise | flops 8192 | bytes 98304 | tf_op jit(solution)/shard_map/add | solution.py:543
Async XLA Ops:
  0.0 32.4 %copy-start = (f32[8,8,128]{2,1,0:T(8,128)S(1)}, f32[8,8,128]{2,1,0:T(8,128)}, u32[]{:S(2)}) copy-start(f32[8,8,128]{2,1,0:T(8,128)} %u_h.1) | copy-start | bytes 98308

commit v3 on v2

--- a/solution.py
+++ b/solution.py
@@ -82,14 +82,12 @@
 
 def lanes(group):
     lane = lax.broadcasted_iota(jnp.int32, (1, 128), 1)
+    block = (lane * 205) >> 11
+    mode = lane - 10 * block
     if group == 0:
-        return lane & 15, lane >> 4
-    inside, low, high = lane < 32, lane < 42, lane < 52
-    element = jnp.where(inside, lane & 15, jnp.where(low, -1, jnp.where(high, 16, 99)))
-    mode = jnp.where(
-        inside, 8 + (lane >> 4), jnp.where(low, lane - 32, jnp.where(high, lane - 42, 99))
-    )
-    return element, mode
+        return jnp.where(lane < 120, block + 1, 99), mode
+    ends = jnp.where(block < 2, block - 1, block + 11)
+    return jnp.where(lane < 60, ends, 99), mode
 
 
 def kernel(
@@ -97,7 +95,7 @@
     u_h, f_h, m_h, eig_h, lam_h, cst_h, out_ref,
     u_v, f_v, m_v, cst_v, ex, eyf, eyb, ez, el, in_sem,
     send_x, send_y, send_d, recv_x, recv_y, recv_d, near_send, near_recv,
-    fe_send, fe_recv, fx_send, fx_recv, far_send, far_recv, ready, pe, px, side_send, side_recv,
+    fe_send, fe_recv, fx_send, fx_recv, far_send, far_recv, ready, near_ready, pe, px, side_send, side_recv,
     xs, xc, cm, cxb, inv, wh, wl, zs,
 ):
     ix, iy, iz = lax.axis_index("gx"), lax.axis_index("gy"), lax.axis_index("gz")
@@ -150,15 +148,25 @@
         target.append((ix + dx, iy + dy, iz))
     barrier = pltpu.get_barrier_semaphore()
     count = jnp.int32(0)
-    greeted = list(zip(near, target)) + [
-        (has_next & ~origin, to_next), (helper, (0, 0, 1)), (after_origin, (0, 0, 0))
+    later = []
+    for dx, dy in DIRS:
+        if dy > 0 or (dy == 0 and dx < 0):
+            later.append(~origin)
+        else:
+            later.append(detour & (iz == 0) & (ix + dx == 0) & (iy + dy == 0))
+    before_me = [ok & ~after for ok, after in zip(near, later)]
+    after_me = [ok & after for ok, after in zip(near, later)]
+    first_row = (iy == 0) & (iz == 0) & (nx > 2)
+    greeted = list(zip(after_me, target)) + [
+        (has_next & ~origin, to_next), (helper, (0, 0, 1)), (after_origin, (0, 0, 0)),
+        (first_row & (ix == nx - 2), (nx - 1, iy, iz)),
     ]
     for ok, device in greeted:
         @pl.when(ok)
         def _(device=device):
             pl.semaphore_signal(barrier, 1, device_id=device, device_id_type=MESH)
     count = jnp.int32(0)
-    for ok in near + [has_prev, origin]:
+    for ok in before_me + [has_prev, origin, first_row & (ix == nx - 1)]:
         count = count + ok.astype(jnp.int32)
 
     ex[:, 10:16, :] = jnp.zeros((10, 6, 16), F32)
@@ -169,6 +177,18 @@
     el[:, 10:16, :] = jnp.zeros((3, 6, 16), F32)
     xs[:, 10:16, :] = jnp.zeros((10, 6, 128), F32)
     xc[96:128, :] = jnp.zeros((32, 128), F32)
+
+    pl.semaphore_wait(barrier, count)
+    for k in range(8):
+        @pl.when(before_me[k])
+        def _(k=k):
+            pl.semaphore_signal(
+                near_ready.at[OPP[k]], 1, device_id=target[k], device_id_type=MESH
+            )
+
+    @pl.when(has_prev & ~after_origin)
+    def _():
+        pl.semaphore_signal(ready, 1, device_id=to_prev, device_id_type=MESH)
 
     for load in loads[:4]:
         load.wait()
@@ -214,10 +234,12 @@
 
     ORDER = [4, 5, 6, 7, 0, 1, 2, 3]
 
-    def send_near(turn):
+    def send_near(turn, where):
         for k in ORDER:
-            @pl.when(near[k])
+            @pl.when(where[k])
             def _(k=k):
+                if where is after_me:
+                    pl.semaphore_wait(near_ready.at[k], 1)
                 outgoing(turn, k).start()
 
     def wait_near(turn):
@@ -239,12 +261,7 @@
                     send_d[turn, k - 4, i, j : j + 1, :] = value[row_x, row_y : row_y + 1]
 
     pack(0, res, (0, 1), (6, 7))
-    pl.semaphore_wait(barrier, count)
-    send_near(0)
-
-    @pl.when(has_prev & ~after_origin)
-    def _():
-        pl.semaphore_signal(ready, 1, device_id=to_prev, device_id_type=MESH)
+    send_near(0, before_me)
 
     for load in loads[4:]:
         load.wait()
@@ -369,6 +386,7 @@
             far_copy(kind, 0, True).wait_recv()
 
     send_down(0)
+    send_near(0, after_me)
     prepare(0)
 
     wait_near(0)
@@ -398,28 +416,7 @@
     def to_modes(g):
         zs[g] = dot3(nodes, (wh[g, 0:128], wl[g, 0:128])).reshape(10, 16, 128)
 
-    to_modes(0)
-
-    @pl.when(has_next & ~origin)
-    def _():
-        pl.semaphore_wait(ready, 1)
-
-    send_up(0)
-    send_up(1)
-    pass_on(0)
-    wait_far(0)
-    prepare(1)
-    to_modes(1)
-    pass_on(1)
-    wait_far(1)
-
-    beyond = halves(fx_recv[...].reshape(32, 128))
-
     def solve(g):
-        more = dot3(beyond, (wh[g, 128:160], wl[g, 128:160]), ((0,), (0,)))
-        zs[g, :, 0:8, :] = zs[g, :, 0:8, :] + more[0:80].reshape(10, 8, 128)
-        for a in range(10):
-            zs[g, a, 8:10, :] = zs[g, a, 8:10, :] + more[80 + 2 * a : 82 + 2 * a]
         value = zs[g].reshape(10, 2, 8, 128)
         total = None
         for a in range(10):
@@ -445,9 +442,31 @@
             halves(total.reshape(160, 128)), (wh[g, 0:128], wl[g, 0:128]), ((1,), (1,))
         )
 
-    found = (solve(0) + solve(1)).reshape(10, 16, 128)
+    to_modes(0)
+
+    @pl.when(has_next & ~origin)
+    def _():
+        pl.semaphore_wait(ready, 1)
+
+    send_up(0)
+    send_up(1)
+    found = solve(0)
+    pass_on(0)
+    wait_far(0)
+    prepare(1)
+    to_modes(1)
+    pass_on(1)
+    wait_far(1)
+
+    beyond = halves(fx_recv[...].reshape(32, 128))
+
+    more = dot3(beyond, (wh[1, 128:160], wl[1, 128:160]), ((0,), (0,)))
+    zs[1, :, 0:8, :] = zs[1, :, 0:8, :] + more[0:80].reshape(10, 8, 128)
+    for a in range(10):
+        zs[1, a, 8:10, :] = zs[1, a, 8:10, :] + more[80 + 2 * a : 82 + 2 * a]
+    found = (found + solve(1)).reshape(10, 16, 128)
     pack(1, found, (8, 0), (7, 9))
-    send_near(1)
+    send_near(1, near)
     wait_near(1)
 
     def gather(own, prev, after):
@@ -489,7 +508,7 @@
         vmem = pltpu.VMEM
         correction = pl.pallas_call(
             functools.partial(kernel, nx, ny, nz),
-            out_shape=jax.ShapeDtypeStruct((8, 8, 128), F32),
+            out_shape=vmem((8, 8, 128), F32),
             in_specs=[hbm] * 6,
             out_specs=pl.BlockSpec(memory_space=vmem),
             scratch_shapes=[
@@ -518,6 +537,7 @@
                 pltpu.SemaphoreType.DMA((2, 2)),
                 pltpu.SemaphoreType.DMA((2, 2)),
                 pltpu.SemaphoreType.REGULAR,
+                pltpu.SemaphoreType.REGULAR((8,)),
                 vmem((1, ROWS), F32),
                 vmem((10, 128), F32),
                 pltpu.SemaphoreType.DMA((2,)),

time: 34.1 us -> 33.3 us (0.977)
  the two profiles are of different devices: /device:TPU:79 before, /device:TPU:119 now
where the time goes in v3:
time: 33.3 us; the launch traced here: 33.1 us
  Pallas kernels  32.5 us (98%)
  other arithmetic  0.62 us (2%)
    pallas_call x1, Pallas kernels, body(): pl.pallas_call(functools.partial(kernel, nx, ny, nz), out_shape=vmem((8,...  32.5 us

profile of v3, /device:TPU:119, one launch (start us, length us, event | category | flops | bytes accessed | tf_op | source)
XLA Modules:
  0.0 33.1 jit_solution(1146883165338561257)
XLA Ops:
  0.0 0.0 copy-start
  0.0 32.5 %shard_map.64 = f32[8,8,128]{2,1,0:T(8,128)S(1)} custom-call(f32[8,8,128]{2,1,0:T(8,128)} %u_h.1, f32[8,8,128]{2,1,0:T(8,128)} %f_h.1, f32[3,8,8,128]{3,2,1,0:T(8,128)} %m_h.1, f32[3,10,10,1,1,16]{5,4,3,2,1,0:T(1,128)} %eig_h.1, f32[3,10,1,1,16]{4,3,2,1,0:T(1,128)} %lam_h.1, bf16[2,448,128]{2,1,0:T(8,128)(2,1)} %constant.2.clone.cst_h), custom_call_target="tpu_custom_call" | custom-call | tf_op jit(solution)/shard_map/pallas_call | solution.py:509
  32.5 0.0 copy-done
  32.5 0.6 %add.3 = f32[8,8,128]{2,1,0:T(8,128)} add(f32[8,8,128]{2,1,0:T(8,128)S(1)} %copy-done, f32[8,8,128]{2,1,0:T(8,128)S(1)} %shard_map.64) | non-fusion elementwise | flops 8192 | bytes 98304 | tf_op jit(solution)/shard_map/add | solution.py:563
Async XLA Ops:
  0.0 32.5 %copy-start = (f32[8,8,128]{2,1,0:T(8,128)S(1)}, f32[8,8,128]{2,1,0:T(8,128)}, u32[]{:S(2)}) copy-start(f32[8,8,128]{2,1,0:T(8,128)} %u_h.1) | copy-start | bytes 98308

commit v4 on v3

--- a/solution.py
+++ b/solution.py
@@ -27,6 +27,8 @@
 
 DIRS = [(-1, 0), (1, 0), (0, -1), (0, 1), (-1, -1), (-1, 1), (1, -1), (1, 1)]
 OPP = [1, 0, 3, 2, 7, 6, 5, 4]
+PIECES = [4, 6, 2, 5, 7, 3, 0, 1, 8]
+HELD = {0: 0, 2: 1, 4: 2, 8: 3}
 OYF, OYB, OZ, OL, ROWS = 160, 320, 480, 720, 768
 
 
@@ -95,7 +97,8 @@
     u_h, f_h, m_h, eig_h, lam_h, cst_h, out_ref,
     u_v, f_v, m_v, cst_v, ex, eyf, eyb, ez, el, in_sem,
     send_x, send_y, send_d, recv_x, recv_y, recv_d, near_send, near_recv,
-    fe_send, fe_recv, fx_send, fx_recv, far_send, far_recv, ready, near_ready, pe, px, side_send, side_recv,
+    fe_send, fe_recv, fx_send, fx_recv, far_send, far_recv, ready, near_ready, pe, side_send, side_recv,
+    slab_send, slab_recv, slab_held, part_send, part_recv, part_held, piece_send, piece_recv, held_send, held_recv, xf, fan,
     xs, xc, cm, cxb, inv, wh, wl, zs,
 ):
     ix, iy, iz = lax.axis_index("gx"), lax.axis_index("gy"), lax.axis_index("gz")
@@ -128,6 +131,10 @@
     recv_d[...] = jnp.zeros_like(recv_d)
     fe_recv[...] = jnp.zeros_like(fe_recv)
     fx_recv[...] = jnp.zeros_like(fx_recv)
+    slab_recv[...] = jnp.zeros_like(slab_recv)
+    part_recv[...] = jnp.zeros_like(part_recv)
+    xf[...] = jnp.zeros_like(xf)
+    fan[...] = jnp.zeros_like(fan)
 
     has_next, has_prev = iz < nz - 1, iz > 0
     to_next, to_prev = (ix, iy, iz + 1), (ix, iy, iz - 1)
@@ -158,15 +165,24 @@
     after_me = [ok & after for ok, after in zip(near, later)]
     first_row = (iy == 0) & (iz == 0) & (nx > 2)
     greeted = list(zip(after_me, target)) + [
-        (has_next & ~origin, to_next), (helper, (0, 0, 1)), (after_origin, (0, 0, 0)),
+        (has_next & ~origin, to_next), (after_origin, (0, 0, 0)),
         (first_row & (ix == nx - 2), (nx - 1, iy, iz)),
     ]
+    over, under, from_origin = [], [], []
+    for k, (dx, dy) in enumerate(DIRS + [(0, 0)]):
+        inside = near[k] if k < 8 else (ix >= 0)
+        over.append(has_next & inside)
+        under.append(has_prev & inside)
+        from_origin.append(detour & (iz == 1) & (ix + dx == 0) & (iy + dy == 0))
+        if k < 8:
+            greeted.append((over[k] & ~origin, (ix + dx, iy + dy, iz + 1)))
     for ok, device in greeted:
         @pl.when(ok)
         def _(device=device):
             pl.semaphore_signal(barrier, 1, device_id=device, device_id_type=MESH)
     count = jnp.int32(0)
-    for ok in before_me + [has_prev, origin, first_row & (ix == nx - 1)]:
+    below = [ok & ~start for ok, start in zip(under, from_origin)]
+    for ok in before_me + below + [origin, first_row & (ix == nx - 1)]:
         count = count + ok.astype(jnp.int32)
 
     ex[:, 10:16, :] = jnp.zeros((10, 6, 16), F32)
@@ -261,6 +277,60 @@
                     send_d[turn, k - 4, i, j : j + 1, :] = value[row_x, row_y : row_y + 1]
 
     pack(0, res, (0, 1), (6, 7))
+    first16 = lax.broadcasted_iota(jnp.int32, (8, 128), 1) < 16
+    low = [jnp.where(first16, res[x], 0.0) for x in range(8)]
+    packed = low[0]
+    for x in range(1, 8):
+        packed = packed + pltpu.roll(low[x], 16 * x, 1)
+    slab_send[...] = packed
+    row8 = lax.broadcasted_iota(jnp.int32, (8, 128), 0)
+    for side, pair in enumerate(((0, 1), (6, 7))):
+        for j, x in enumerate(pair):
+            line = jnp.where(row8 == 0, low[x], 0.0)
+            for y in range(1, 8):
+                line = line + jnp.where(row8 == y, pltpu.roll(low[x], 16 * y, 1), 0.0)
+            part_send[side, j : j + 1, :] = line.sum(axis=0, keepdims=True)
+
+    def piece(k, arriving, held=False):
+        dx, dy = (DIRS + [(0, 0)])[k]
+        if k == 8:
+            src, slot, dst = slab_send, 8, slab_recv
+        else:
+            slot = k if arriving else OPP[k]
+            src = part_send.at[k] if k < 2 else slab_send.at[pl.ds(6 if dy > 0 else 0, 2)]
+            dst = part_recv.at[slot]
+        if held:
+            dst = slab_held if k == 8 else part_held.at[HELD[k]]
+        return pltpu.make_async_remote_copy(
+            src_ref=src,
+            dst_ref=dst,
+            send_sem=piece_send.at[k],
+            recv_sem=held_recv.at[HELD[k]] if held else piece_recv.at[slot],
+            device_id=(1, 0, 0) if held else (ix + dx, iy + dy, iz + 1 if arriving else iz - 1),
+            device_id_type=MESH,
+        )
+
+    def pass_piece(k):
+        slot = 8 if k == 8 else OPP[k]
+        return pltpu.make_async_remote_copy(
+            src_ref=slab_held if k == 8 else part_held.at[HELD[k]],
+            dst_ref=slab_recv if k == 8 else part_recv.at[slot],
+            send_sem=held_send.at[HELD[k]],
+            recv_sem=piece_recv.at[slot],
+            device_id=(0, 0, 0),
+            device_id_type=MESH,
+        )
+
+    for k in PIECES:
+        @pl.when(below[k])
+        def _(k=k):
+            piece(k, False).start()
+
+        if k in HELD:
+            @pl.when(under[k] & from_origin[k])
+            def _(k=k):
+                piece(k, False, True).start()
+
     send_near(0, before_me)
 
     for load in loads[4:]:
@@ -324,14 +394,11 @@
             some = rate > 0.0
             inv[g, p] = jnp.where(some, 1.0 / jnp.where(some, rate, 1.0), 0.0)
 
-    def rows_of(way):
-        return pl.ds(6, 10) if way == 0 else pl.ds(0, 10)
-
     def far_copy(kind, way, arriving):
         if kind == 0:
             src, dst = fe_send.at[1 - way], fe_recv.at[way]
         else:
-            src, dst = fx_send.at[way, rows_of(way)], fx_recv.at[way, rows_of(way)]
+            src, dst = fx_send.at[pl.ds(6, 10)], fx_recv.at[pl.ds(6, 10)]
         return pltpu.make_async_remote_copy(
             src_ref=src,
             dst_ref=dst,
@@ -341,51 +408,29 @@
             device_id_type=MESH,
         )
 
-    def aside(kind, passing):
-        held = pe if kind == 0 else px
-        if passing:
-            src, dst = held, fe_recv.at[1] if kind == 0 else fx_recv.at[1, rows_of(1)]
-        else:
-            src, dst = fe_send.at[0] if kind == 0 else fx_send.at[1, rows_of(1)], held
+    def aside(passing):
         return pltpu.make_async_remote_copy(
-            src_ref=src,
-            dst_ref=dst,
-            send_sem=side_send.at[kind] if passing else far_send.at[kind, 1],
-            recv_sem=far_recv.at[kind, 1] if passing else side_recv.at[kind],
+            src_ref=pe if passing else fe_send.at[0],
+            dst_ref=fe_recv.at[1] if passing else pe,
+            send_sem=side_send if passing else far_send.at[0, 1],
+            recv_sem=far_recv.at[0, 1] if passing else side_recv,
             device_id=(0, 0, 0) if passing else (1, 0, 0),
             device_id_type=MESH,
         )
 
-    def send_down(kind):
-        @pl.when(has_prev & ~after_origin)
-        def _():
-            far_copy(kind, 1, False).start()
-
-        @pl.when(after_origin)
-        def _():
-            aside(kind, False).start()
+    @pl.when(below[8])
+    def _():
+        far_copy(0, 1, False).start()
+
+    @pl.when(after_origin)
+    def _():
+        aside(False).start()
 
     def send_up(kind):
         @pl.when(has_next)
         def _():
             far_copy(kind, 0, False).start()
 
-    def pass_on(kind):
-        @pl.when(helper)
-        def _():
-            aside(kind, False).wait_recv()
-            aside(kind, True).start()
-
-    def wait_far(kind):
-        @pl.when(has_next)
-        def _():
-            far_copy(kind, 1, True).wait_recv()
-
-        @pl.when(has_prev)
-        def _():
-            far_copy(kind, 0, True).wait_recv()
-
-    send_down(0)
     send_near(0, after_me)
     prepare(0)
 
@@ -407,10 +452,8 @@
     for a in range(10):
         xc[80 + 2 * a : 82 + 2 * a, :] = xs[a, 8:10, :]
     turned = xc[...].T
-    fx_send[0] = turned[112:128]
-    fx_send[1] = turned[0:16]
-
-    send_down(1)
+    fx_send[...] = turned[112:128]
+
     nodes = halves(xs[...].reshape(160, 128))
 
     def to_modes(g):
@@ -451,16 +494,71 @@
     send_up(0)
     send_up(1)
     found = solve(0)
-    pass_on(0)
-    wait_far(0)
+
+    @pl.when(helper)
+    def _():
+        aside(False).wait_recv()
+        aside(True).start()
+
+    @pl.when(has_next)
+    def _():
+        far_copy(0, 1, True).wait_recv()
+
+    @pl.when(has_prev)
+    def _():
+        far_copy(0, 0, True).wait_recv()
+
     prepare(1)
     to_modes(1)
-    pass_on(1)
-    wait_far(1)
-
-    beyond = halves(fx_recv[...].reshape(32, 128))
-
-    more = dot3(beyond, (wh[1, 128:160], wl[1, 128:160]), ((0,), (0,)))
+
+    @pl.when(helper)
+    def _():
+        for k in HELD:
+            piece(k, False, True).wait_recv()
+            pass_piece(k).start()
+
+    @pl.when(has_prev)
+    def _():
+        far_copy(1, 0, True).wait_recv()
+
+    for k in PIECES:
+        @pl.when(over[k])
+        def _(k=k):
+            piece(k, True).wait_recv()
+
+    def unpack(rows):
+        return jnp.concatenate(
+            [(pltpu.roll(rows, 128 - 16 * x, 1) if x else rows)[None] for x in range(8)], axis=0
+        )
+
+    own = unpack(slab_recv[...])
+    sides = []
+    for side in range(2):
+        lines = []
+        for j in range(2):
+            line = jnp.broadcast_to(part_recv[side, j : j + 1, :], (8, 128))
+            tile = jnp.where(row8 == 0, line, 0.0)
+            for y in range(1, 8):
+                tile = tile + jnp.where(row8 == y, pltpu.roll(line, 128 - 16 * y, 1), 0.0)
+            lines.append(tile[None])
+        sides.append(jnp.concatenate(lines, axis=0))
+    for i in range(6):
+        fan[2 * i : 2 * i + 2, :] = part_recv[2 + i]
+    wide = unpack(fan[...])
+    xf[:, 0:8, :] = join(own, sides[0], sides[1])
+    before = join(wide[:, 0:2], wide[6:8, 4:6], wide[0:2, 8:10])
+    behind = join(wide[:, 2:4], wide[6:8, 6:8], wide[0:2, 10:12])
+    xf[:, 0:1, :] = xf[:, 0:1, :] + before[:, 1:2]
+    xf[:, 7:8, :] = xf[:, 7:8, :] + behind[:, 0:1]
+    xf[:, 8:9, :] = before[:, 0:1]
+    xf[:, 9:10, :] = behind[:, 1:2]
+    above = halves(xf[:, :, 0:16].reshape(160, 16))
+    risen = dot3(above, (wh[1, 144:160], wl[1, 144:160])).reshape(10, 16, 128)
+
+    beyond = halves(fx_recv[...])
+
+    more = dot3(beyond, (wh[1, 128:144], wl[1, 128:144]), ((0,), (0,)))
+    zs[1] = zs[1] + risen
     zs[1, :, 0:8, :] = zs[1, :, 0:8, :] + more[0:80].reshape(10, 8, 128)
     for a in range(10):
         zs[1, a, 8:10, :] = zs[1, a, 8:10, :] + more[80 + 2 * a : 82 + 2 * a]
@@ -487,17 +585,24 @@
         def _(kind=kind):
             far_copy(kind, 0, False).wait_send()
 
-        @pl.when(has_prev & ~after_origin)
-        def _(kind=kind):
-            far_copy(kind, 1, False).wait_send()
-
-        @pl.when(after_origin)
-        def _(kind=kind):
-            aside(kind, False).wait_send()
-
-        @pl.when(helper)
-        def _(kind=kind):
-            aside(kind, True).wait_send()
+    @pl.when(below[8])
+    def _():
+        far_copy(0, 1, False).wait_send()
+
+    @pl.when(after_origin)
+    def _():
+        aside(False).wait_send()
+
+    @pl.when(helper)
+    def _():
+        aside(True).wait_send()
+        for k in HELD:
+            pass_piece(k).wait_send()
+
+    for k in PIECES:
+        @pl.when(under[k])
+        def _(k=k):
+            piece(k, False).wait_send()
 
 
 def solution(mesh):
@@ -532,16 +637,27 @@
                 pltpu.SemaphoreType.DMA((2, 8)),
                 vmem((2, 1, ROWS), F32),
                 vmem((2, 1, ROWS), F32),
-                vmem((2, 16, 128), F32),
-                vmem((2, 16, 128), F32),
+                vmem((16, 128), F32),
+                vmem((16, 128), F32),
                 pltpu.SemaphoreType.DMA((2, 2)),
                 pltpu.SemaphoreType.DMA((2, 2)),
                 pltpu.SemaphoreType.REGULAR,
                 pltpu.SemaphoreType.REGULAR((8,)),
                 vmem((1, ROWS), F32),
-                vmem((10, 128), F32),
-                pltpu.SemaphoreType.DMA((2,)),
-                pltpu.SemaphoreType.DMA((2,)),
+                pltpu.SemaphoreType.DMA,
+                pltpu.SemaphoreType.DMA,
+                vmem((8, 128), F32),
+                vmem((8, 128), F32),
+                vmem((8, 128), F32),
+                vmem((2, 2, 128), F32),
+                vmem((8, 2, 128), F32),
+                vmem((3, 2, 128), F32),
+                pltpu.SemaphoreType.DMA((9,)),
+                pltpu.SemaphoreType.DMA((9,)),
+                pltpu.SemaphoreType.DMA((4,)),
+                pltpu.SemaphoreType.DMA((4,)),
+                vmem((10, 16, 128), F32),
+                vmem((16, 128), F32),
                 vmem((10, 16, 128), F32),
                 vmem((128, 128), F32),
                 vmem((2, ROWS, 128), F32),

time: 33.3 us -> 30.2 us (0.907)
  the two profiles are of different devices: /device:TPU:119 before, /device:TPU:879 now
where the time goes in v4:
time: 30.2 us; the launch traced here: 30 us
  Pallas kernels  29.4 us (97%)
  other arithmetic  0.62 us (2%)
    pallas_call x1, Pallas kernels, body(): pl.pallas_call(functools.partial(kernel, nx, ny, nz), out_shape=vmem((8,...  29.4 us
    add x1, other arithmetic, body(): return initial + correction  0.62 us

profile of v4, /device:TPU:879, one launch (start us, length us, event | category | flops | bytes accessed | tf_op | source)
XLA Modules:
  0.0 30.0 jit_solution(2304811483999147337)
XLA Ops:
  0.0 0.0 copy-start
  0.0 29.4 %shard_map.64 = f32[8,8,128]{2,1,0:T(8,128)S(1)} custom-call(f32[8,8,128]{2,1,0:T(8,128)} %u_h.1, f32[8,8,128]{2,1,0:T(8,128)} %f_h.1, f32[3,8,8,128]{3,2,1,0:T(8,128)} %m_h.1, f32[3,10,10,1,1,16]{5,4,3,2,1,0:T(1,128)} %eig_h.1, f32[3,10,1,1,16]{4,3,2,1,0:T(1,128)} %lam_h.1, bf16[2,448,128]{2,1,0:T(8,128)(2,1)} %constant.2.clone.cst_h), custom_call_target="tpu_custom_call" | custom-call | tf_op jit(solution)/shard_map/pallas_call | solution.py:614
  29.4 0.0 copy-done
  29.4 0.6 %add.3 = f32[8,8,128]{2,1,0:T(8,128)} add(f32[8,8,128]{2,1,0:T(8,128)S(1)} %copy-done, f32[8,8,128]{2,1,0:T(8,128)S(1)} %shard_map.64) | non-fusion elementwise | flops 8192 | bytes 98304 | tf_op jit(solution)/shard_map/add | solution.py:679
Async XLA Ops:
  0.0 29.4 %copy-start = (f32[8,8,128]{2,1,0:T(8,128)S(1)}, f32[8,8,128]{2,1,0:T(8,128)}, u32[]{:S(2)}) copy-start(f32[8,8,128]{2,1,0:T(8,128)} %u_h.1) | copy-start | bytes 98308

commit v5 on v4

--- a/solution.py
+++ b/solution.py
@@ -168,6 +168,14 @@
         (has_next & ~origin, to_next), (after_origin, (0, 0, 0)),
         (first_row & (ix == nx - 2), (nx - 1, iy, iz)),
     ]
+    spot, half = iz * ny + iy, max(ny // 2, 1)
+    relayed = nz > 2
+    last, second = relayed & (iz == nz - 1), relayed & (iz == nz - 2)
+    middle = relayed & (spot >= (nz - 2) * ny + half) & (spot < (nz - 1) * ny + half)
+    down_spot, up_spot = jnp.maximum(spot - half, 0), spot + half
+    half_down = (ix, down_spot % ny, down_spot // ny)
+    half_up = (ix, up_spot % ny, up_spot // ny)
+    greeted += [(last, half_down), (second, half_up)]
     over, under, from_origin = [], [], []
     for k, (dx, dy) in enumerate(DIRS + [(0, 0)]):
         inside = near[k] if k < 8 else (ix >= 0)
@@ -184,6 +192,7 @@
     below = [ok & ~start for ok, start in zip(under, from_origin)]
     for ok in before_me + below + [origin, first_row & (ix == nx - 1)]:
         count = count + ok.astype(jnp.int32)
+    count = count + 2 * middle.astype(jnp.int32)
 
     ex[:, 10:16, :] = jnp.zeros((10, 6, 16), F32)
     eyf[:, 10:16, :] = jnp.zeros((10, 6, 16), F32)
@@ -202,9 +211,13 @@
                 near_ready.at[OPP[k]], 1, device_id=target[k], device_id_type=MESH
             )
 
-    @pl.when(has_prev & ~after_origin)
+    @pl.when(has_prev & ~after_origin & ~last)
     def _():
         pl.semaphore_signal(ready, 1, device_id=to_prev, device_id_type=MESH)
+
+    @pl.when(middle)
+    def _():
+        pl.semaphore_signal(ready, 1, device_id=half_down, device_id_type=MESH)
 
     for load in loads[:4]:
         load.wait()
@@ -276,21 +289,12 @@
                 for j, row_y in enumerate(rows_y):
                     send_d[turn, k - 4, i, j : j + 1, :] = value[row_x, row_y : row_y + 1]
 
-    pack(0, res, (0, 1), (6, 7))
     first16 = lax.broadcasted_iota(jnp.int32, (8, 128), 1) < 16
     low = [jnp.where(first16, res[x], 0.0) for x in range(8)]
     packed = low[0]
     for x in range(1, 8):
         packed = packed + pltpu.roll(low[x], 16 * x, 1)
     slab_send[...] = packed
-    row8 = lax.broadcasted_iota(jnp.int32, (8, 128), 0)
-    for side, pair in enumerate(((0, 1), (6, 7))):
-        for j, x in enumerate(pair):
-            line = jnp.where(row8 == 0, low[x], 0.0)
-            for y in range(1, 8):
-                line = line + jnp.where(row8 == y, pltpu.roll(low[x], 16 * y, 1), 0.0)
-            part_send[side, j : j + 1, :] = line.sum(axis=0, keepdims=True)
-
     def piece(k, arriving, held=False):
         dx, dy = (DIRS + [(0, 0)])[k]
         if k == 8:
@@ -321,16 +325,28 @@
             device_id_type=MESH,
         )
 
-    for k in PIECES:
-        @pl.when(below[k])
-        def _(k=k):
-            piece(k, False).start()
-
-        if k in HELD:
-            @pl.when(under[k] & from_origin[k])
+    def send_pieces(pieces):
+        for k in pieces:
+            @pl.when(below[k])
             def _(k=k):
-                piece(k, False, True).start()
-
+                piece(k, False).start()
+
+            if k in HELD:
+                @pl.when(under[k] & from_origin[k])
+                def _(k=k):
+                    piece(k, False, True).start()
+
+    send_pieces([k for k in PIECES if k > 1])
+    row8 = lax.broadcasted_iota(jnp.int32, (8, 128), 0)
+    for side, pair in enumerate(((0, 1), (6, 7))):
+        for j, x in enumerate(pair):
+            line = jnp.where(row8 == 0, low[x], 0.0)
+            for y in range(1, 8):
+                line = line + jnp.where(row8 == y, pltpu.roll(low[x], 16 * y, 1), 0.0)
+            part_send[side, j : j + 1, :] = line.sum(axis=0, keepdims=True)
+
+    send_pieces([k for k in PIECES if k < 2])
+    pack(0, res, (0, 1), (6, 7))
     send_near(0, before_me)
 
     for load in loads[4:]:
@@ -565,14 +581,6 @@
     found = (found + solve(1)).reshape(10, 16, 128)
     pack(1, found, (8, 0), (7, 9))
     send_near(1, near)
-    wait_near(1)
-
-    def gather(own, prev, after):
-        return jnp.concatenate([own[0:2] + prev, own[2:6], own[6:8] + after], axis=0)
-
-    out_ref[...] = gather(found[0:8, 0:8], recv_x[1, 0], recv_x[1, 1])
-    out_ref[:, 0:2, :] = out_ref[:, 0:2, :] + gather(recv_y[1, 0], recv_d[1, 0], recv_d[1, 2])
-    out_ref[:, 6:8, :] = out_ref[:, 6:8, :] + gather(recv_y[1, 1], recv_d[1, 1], recv_d[1, 3])
 
     for turn in range(2):
         for k in range(8):
@@ -603,6 +611,15 @@
         @pl.when(under[k])
         def _(k=k):
             piece(k, False).wait_send()
+
+    wait_near(1)
+
+    def gather(own, prev, after):
+        return jnp.concatenate([own[0:2] + prev, own[2:6], own[6:8] + after], axis=0)
+
+    out_ref[...] = gather(found[0:8, 0:8], recv_x[1, 0], recv_x[1, 1])
+    out_ref[:, 0:2, :] = out_ref[:, 0:2, :] + gather(recv_y[1, 0], recv_d[1, 0], recv_d[1, 2])
+    out_ref[:, 6:8, :] = out_ref[:, 6:8, :] + gather(recv_y[1, 1], recv_d[1, 1], recv_d[1, 3])
 
 
 def solution(mesh):

time: 30.2 us -> 29.6 us (0.980)
  the two profiles are of different devices: /device:TPU:879 before, /device:TPU:120 now
where the time goes in v5:
time: 29.6 us; the launch traced here: 29.5 us
  Pallas kernels  28.8 us (97%)
  other arithmetic  0.62 us (2%)
    pallas_call x1, Pallas kernels, body(): pl.pallas_call(functools.partial(kernel, nx, ny, nz), out_shape=vmem((8,...  28.8 us
    add x1, other arithmetic, body(): return initial + correction  0.62 us

profile of v5, /device:TPU:120, one launch (start us, length us, event | category | flops | bytes accessed | tf_op | source)
XLA Modules:
  0.0 29.5 jit_solution(16476390676798673753)
XLA Ops:
  0.0 0.0 copy-start
  0.0 28.8 %shard_map.64 = f32[8,8,128]{2,1,0:T(8,128)S(1)} custom-call(f32[8,8,128]{2,1,0:T(8,128)} %u_h.1, f32[8,8,128]{2,1,0:T(8,128)} %f_h.1, f32[3,8,8,128]{3,2,1,0:T(8,128)} %m_h.1, f32[3,10,10,1,1,16]{5,4,3,2,1,0:T(1,128)} %eig_h.1, f32[3,10,1,1,16]{4,3,2,1,0:T(1,128)} %lam_h.1, bf16[2,448,128]{2,1,0:T(8,128)(2,1)} %constant.2.clone.cst_h), custom_call_target="tpu_custom_call" | custom-call | tf_op jit(solution)/shard_map/pallas_call | solution.py:631
  28.8 0.0 copy-done
  28.8 0.6 %add.3 = f32[8,8,128]{2,1,0:T(8,128)} add(f32[8,8,128]{2,1,0:T(8,128)S(1)} %copy-done, f32[8,8,128]{2,1,0:T(8,128)S(1)} %shard_map.64) | non-fusion elementwise | flops 8192 | bytes 98304 | tf_op jit(solution)/shard_map/add | solution.py:696
Async XLA Ops:
  0.0 28.8 %copy-start = (f32[8,8,128]{2,1,0:T(8,128)S(1)}, f32[8,8,128]{2,1,0:T(8,128)}, u32[]{:S(2)}) copy-start(f32[8,8,128]{2,1,0:T(8,128)} %u_h.1) | copy-start | bytes 98308

commit v6 on v5

--- a/solution.py
+++ b/solution.py
@@ -133,8 +133,6 @@
     fx_recv[...] = jnp.zeros_like(fx_recv)
     slab_recv[...] = jnp.zeros_like(slab_recv)
     part_recv[...] = jnp.zeros_like(part_recv)
-    xf[...] = jnp.zeros_like(xf)
-    fan[...] = jnp.zeros_like(fan)
 
     has_next, has_prev = iz < nz - 1, iz > 0
     to_next, to_prev = (ix, iy, iz + 1), (ix, iy, iz - 1)
@@ -161,8 +159,9 @@
             later.append(~origin)
         else:
             later.append(detour & (iz == 0) & (ix + dx == 0) & (iy + dy == 0))
-    before_me = [ok & ~after for ok, after in zip(near, later)]
-    after_me = [ok & after for ok, after in zip(near, later)]
+    beside = [near[k] & (iz > 0) & (iy < ny - 1) & (DIRS[k][1] == 0) for k in range(8)]
+    before_me = [ok & ~after & ~x for ok, after, x in zip(near, later, beside)]
+    after_me = [ok & after & ~x for ok, after, x in zip(near, later, beside)]
     first_row = (iy == 0) & (iz == 0) & (nx > 2)
     greeted = list(zip(after_me, target)) + [
         (has_next & ~origin, to_next), (after_origin, (0, 0, 0)),
@@ -194,6 +193,8 @@
         count = count + ok.astype(jnp.int32)
     count = count + 2 * middle.astype(jnp.int32)
 
+    xf[...] = jnp.zeros_like(xf)
+    fan[...] = jnp.zeros_like(fan)
     ex[:, 10:16, :] = jnp.zeros((10, 6, 16), F32)
     eyf[:, 10:16, :] = jnp.zeros((10, 6, 16), F32)
     eyb[:, 10:16, :] = jnp.zeros((10, 6, 16), F32)
@@ -202,22 +203,6 @@
     el[:, 10:16, :] = jnp.zeros((3, 6, 16), F32)
     xs[:, 10:16, :] = jnp.zeros((10, 6, 128), F32)
     xc[96:128, :] = jnp.zeros((32, 128), F32)
-
-    pl.semaphore_wait(barrier, count)
-    for k in range(8):
-        @pl.when(before_me[k])
-        def _(k=k):
-            pl.semaphore_signal(
-                near_ready.at[OPP[k]], 1, device_id=target[k], device_id_type=MESH
-            )
-
-    @pl.when(has_prev & ~after_origin & ~last)
-    def _():
-        pl.semaphore_signal(ready, 1, device_id=to_prev, device_id_type=MESH)
-
-    @pl.when(middle)
-    def _():
-        pl.semaphore_signal(ready, 1, device_id=half_down, device_id_type=MESH)
 
     for load in loads[:4]:
         load.wait()
@@ -336,7 +321,23 @@
                 def _(k=k):
                     piece(k, False, True).start()
 
+    pl.semaphore_wait(barrier, count)
     send_pieces([k for k in PIECES if k > 1])
+    for k in range(8):
+        @pl.when(before_me[k])
+        def _(k=k):
+            pl.semaphore_signal(
+                near_ready.at[OPP[k]], 1, device_id=target[k], device_id_type=MESH
+            )
+
+    @pl.when(has_prev & ~after_origin & ~last)
+    def _():
+        pl.semaphore_signal(ready, 1, device_id=to_prev, device_id_type=MESH)
+
+    @pl.when(middle)
+    def _():
+        pl.semaphore_signal(ready, 1, device_id=half_down, device_id_type=MESH)
+
     row8 = lax.broadcasted_iota(jnp.int32, (8, 128), 0)
     for side, pair in enumerate(((0, 1), (6, 7))):
         for j, x in enumerate(pair):
@@ -448,6 +449,7 @@
             far_copy(kind, 0, False).start()
 
     send_near(0, after_me)
+    send_near(0, beside)
     prepare(0)
 
     wait_near(0)

time: 29.6 us -> 29.2 us (0.986)
  Pallas kernels: 28.8 us -> 28.4 us
    pallas_call x1, Pallas kernels: 28.8 us -> 28.4 us  [body(): pl.pallas_call(functools.partial(kernel, nx, ny, nz), out_shape=vmem((8,...]
where the time goes in v6:
time: 29.2 us; the launch traced here: 29 us
  Pallas kernels  28.4 us (97%)
  other arithmetic  0.62 us (2%)
    pallas_call x1, Pallas kernels, body(): pl.pallas_call(functools.partial(kernel, nx, ny, nz), out_shape=vmem((8,...  28.4 us
    add x1, other arithmetic, body(): return initial + correction  0.62 us

profile of v6, /device:TPU:120, one launch (start us, length us, event | category | flops | bytes accessed | tf_op | source)
XLA Modules:
  0.0 29.0 jit_solution(13542714364902308022)
XLA Ops:
  0.0 0.0 copy-start
  0.0 28.4 %shard_map.64 = f32[8,8,128]{2,1,0:T(8,128)S(1)} custom-call(f32[8,8,128]{2,1,0:T(8,128)} %u_h.1, f32[8,8,128]{2,1,0:T(8,128)} %f_h.1, f32[3,8,8,128]{3,2,1,0:T(8,128)} %m_h.1, f32[3,10,10,1,1,16]{5,4,3,2,1,0:T(1,128)} %eig_h.1, f32[3,10,1,1,16]{4,3,2,1,0:T(1,128)} %lam_h.1, bf16[2,448,128]{2,1,0:T(8,128)(2,1)} %constant.2.clone.cst_h), custom_call_target="tpu_custom_call" | custom-call | tf_op jit(solution)/shard_map/pallas_call | solution.py:633
  28.4 0.0 copy-done
  28.4 0.6 %add.3 = f32[8,8,128]{2,1,0:T(8,128)} add(f32[8,8,128]{2,1,0:T(8,128)S(1)} %copy-done, f32[8,8,128]{2,1,0:T(8,128)S(1)} %shard_map.64) | non-fusion elementwise | flops 8192 | bytes 98304 | tf_op jit(solution)/shard_map/add | solution.py:698
Async XLA Ops:
  0.0 28.4 %copy-start = (f32[8,8,128]{2,1,0:T(8,128)S(1)}, f32[8,8,128]{2,1,0:T(8,128)}, u32[]{:S(2)}) copy-start(f32[8,8,128]{2,1,0:T(8,128)} %u_h.1) | copy-start | bytes 98308

commit v7 on v6

--- a/solution.py
+++ b/solution.py
@@ -248,8 +248,8 @@
 
     ORDER = [4, 5, 6, 7, 0, 1, 2, 3]
 
-    def send_near(turn, where):
-        for k in ORDER:
+    def send_near(turn, where, order=ORDER):
+        for k in order:
             @pl.when(where[k])
             def _(k=k):
                 if where is after_me:
@@ -262,11 +262,13 @@
             def _(k=k):
                 incoming(turn, k).wait_recv()
 
-    def pack(turn, value, low, high):
+    def pack_sides(turn, value, low, high):
         for side, rows in enumerate((low, high)):
             for j, row in enumerate(rows):
                 send_x[turn, side, j] = value[row, 0:8]
                 send_y[turn, side, :, j : j + 1, :] = value[0:8, row : row + 1]
+
+    def pack_corners(turn, value, low, high):
         for k in range(4, 8):
             rows_x = low if DIRS[k][0] < 0 else high
             rows_y = low if DIRS[k][1] < 0 else high
@@ -347,7 +349,8 @@
             part_send[side, j : j + 1, :] = line.sum(axis=0, keepdims=True)
 
     send_pieces([k for k in PIECES if k < 2])
-    pack(0, res, (0, 1), (6, 7))
+    pack_corners(0, res, (0, 1), (6, 7))
+    pack_sides(0, res, (0, 1), (6, 7))
     send_near(0, before_me)
 
     for load in loads[4:]:
@@ -539,6 +542,13 @@
     def _():
         far_copy(1, 0, True).wait_recv()
 
+    beyond = halves(fx_recv[...])
+
+    more = dot3(beyond, (wh[1, 128:144], wl[1, 128:144]), ((0,), (0,)))
+    zs[1, :, 0:8, :] = zs[1, :, 0:8, :] + more[0:80].reshape(10, 8, 128)
+    for a in range(10):
+        zs[1, a, 8:10, :] = zs[1, a, 8:10, :] + more[80 + 2 * a : 82 + 2 * a]
+
     for k in PIECES:
         @pl.when(over[k])
         def _(k=k):
@@ -573,16 +583,12 @@
     above = halves(xf[:, :, 0:16].reshape(160, 16))
     risen = dot3(above, (wh[1, 144:160], wl[1, 144:160])).reshape(10, 16, 128)
 
-    beyond = halves(fx_recv[...])
-
-    more = dot3(beyond, (wh[1, 128:144], wl[1, 128:144]), ((0,), (0,)))
     zs[1] = zs[1] + risen
-    zs[1, :, 0:8, :] = zs[1, :, 0:8, :] + more[0:80].reshape(10, 8, 128)
-    for a in range(10):
-        zs[1, a, 8:10, :] = zs[1, a, 8:10, :] + more[80 + 2 * a : 82 + 2 * a]
     found = (found + solve(1)).reshape(10, 16, 128)
-    pack(1, found, (8, 0), (7, 9))
-    send_near(1, near)
+    pack_corners(1, found, (8, 0), (7, 9))
+    send_near(1, near, ORDER[:4])
+    pack_sides(1, found, (8, 0), (7, 9))
+    send_near(1, near, ORDER[4:])
 
     for turn in range(2):
         for k in range(8):

time: 29.2 us -> 29.1 us (level)
  no operation moved by 1% of the time
where the time goes in v7:
time: 29.1 us; the launch traced here: 28.9 us
  Pallas kernels  28.3 us (97%)
  other arithmetic  0.62 us (2%)
    pallas_call x1, Pallas kernels, body(): pl.pallas_call(functools.partial(kernel, nx, ny, nz), out_shape=vmem((8,...  28.3 us
    add x1, other arithmetic, body(): return initial + correction  0.62 us

profile of v7, /device:TPU:120, one launch (start us, length us, event | category | flops | bytes accessed | tf_op | source)
XLA Modules:
  0.0 28.9 jit_solution(8643913707315416053)
XLA Ops:
  0.0 0.0 copy-start
  0.0 28.3 %shard_map.64 = f32[8,8,128]{2,1,0:T(8,128)S(1)} custom-call(f32[8,8,128]{2,1,0:T(8,128)} %u_h.1, f32[8,8,128]{2,1,0:T(8,128)} %f_h.1, f32[3,8,8,128]{3,2,1,0:T(8,128)} %m_h.1, f32[3,10,10,1,1,16]{5,4,3,2,1,0:T(1,128)} %eig_h.1, f32[3,10,1,1,16]{4,3,2,1,0:T(1,128)} %lam_h.1, bf16[2,448,128]{2,1,0:T(8,128)(2,1)} %constant.2.clone.cst_h), custom_call_target="tpu_custom_call" | custom-call | tf_op jit(solution)/shard_map/pallas_call | solution.py:639
  28.3 0.0 copy-done
  28.3 0.6 %add.3 = f32[8,8,128]{2,1,0:T(8,128)} add(f32[8,8,128]{2,1,0:T(8,128)S(1)} %copy-done, f32[8,8,128]{2,1,0:T(8,128)S(1)} %shard_map.64) | non-fusion elementwise | flops 8192 | bytes 98304 | tf_op jit(solution)/shard_map/add | solution.py:704
Async XLA Ops:
  0.0 28.3 %copy-start = (f32[8,8,128]{2,1,0:T(8,128)S(1)}, f32[8,8,128]{2,1,0:T(8,128)}, u32[]{:S(2)}) copy-start(f32[8,8,128]{2,1,0:T(8,128)} %u_h.1) | copy-start | bytes 98308

commit v8 on v6

--- a/solution.py
+++ b/solution.py
@@ -539,6 +539,13 @@
     def _():
         far_copy(1, 0, True).wait_recv()
 
+    beyond = halves(fx_recv[...])
+
+    more = dot3(beyond, (wh[1, 128:144], wl[1, 128:144]), ((0,), (0,)))
+    zs[1, :, 0:8, :] = zs[1, :, 0:8, :] + more[0:80].reshape(10, 8, 128)
+    for a in range(10):
+        zs[1, a, 8:10, :] = zs[1, a, 8:10, :] + more[80 + 2 * a : 82 + 2 * a]
+
     for k in PIECES:
         @pl.when(over[k])
         def _(k=k):
@@ -573,13 +580,7 @@
     above = halves(xf[:, :, 0:16].reshape(160, 16))
     risen = dot3(above, (wh[1, 144:160], wl[1, 144:160])).reshape(10, 16, 128)
 
-    beyond = halves(fx_recv[...])
-
-    more = dot3(beyond, (wh[1, 128:144], wl[1, 128:144]), ((0,), (0,)))
     zs[1] = zs[1] + risen
-    zs[1, :, 0:8, :] = zs[1, :, 0:8, :] + more[0:80].reshape(10, 8, 128)
-    for a in range(10):
-        zs[1, a, 8:10, :] = zs[1, a, 8:10, :] + more[80 + 2 * a : 82 + 2 * a]
     found = (found + solve(1)).reshape(10, 16, 128)
     pack(1, found, (8, 0), (7, 9))
     send_near(1, near)

time: 29.2 us -> 29.1 us (level)
  no operation moved by 1% of the time
where the time goes in v8:
time: 29.1 us; the launch traced here: 28.9 us
  Pallas kernels  28.3 us (97%)
  other arithmetic  0.62 us (2%)
    pallas_call x1, Pallas kernels, body(): pl.pallas_call(functools.partial(kernel, nx, ny, nz), out_shape=vmem((8,...  28.3 us
    add x1, other arithmetic, body(): return initial + correction  0.62 us

profile of v8, /device:TPU:120, one launch (start us, length us, event | category | flops | bytes accessed | tf_op | source)
XLA Modules:
  0.0 28.9 jit_solution(12358501333567646147)
XLA Ops:
  0.0 0.0 copy-start
  0.0 28.3 %shard_map.64 = f32[8,8,128]{2,1,0:T(8,128)S(1)} custom-call(f32[8,8,128]{2,1,0:T(8,128)} %u_h.1, f32[8,8,128]{2,1,0:T(8,128)} %f_h.1, f32[3,8,8,128]{3,2,1,0:T(8,128)} %m_h.1, f32[3,10,10,1,1,16]{5,4,3,2,1,0:T(1,128)} %eig_h.1, f32[3,10,1,1,16]{4,3,2,1,0:T(1,128)} %lam_h.1, bf16[2,448,128]{2,1,0:T(8,128)(2,1)} %constant.2.clone.cst_h), custom_call_target="tpu_custom_call" | custom-call | tf_op jit(solution)/shard_map/pallas_call | solution.py:634
  28.3 0.0 copy-done
  28.3 0.6 %add.3 = f32[8,8,128]{2,1,0:T(8,128)} add(f32[8,8,128]{2,1,0:T(8,128)S(1)} %copy-done, f32[8,8,128]{2,1,0:T(8,128)S(1)} %shard_map.64) | non-fusion elementwise | flops 8192 | bytes 98304 | tf_op jit(solution)/shard_map/add | solution.py:699
Async XLA Ops:
  0.0 28.3 %copy-start = (f32[8,8,128]{2,1,0:T(8,128)S(1)}, f32[8,8,128]{2,1,0:T(8,128)}, u32[]{:S(2)}) copy-start(f32[8,8,128]{2,1,0:T(8,128)} %u_h.1) | copy-start | bytes 98308
